TPU v7x, 256 devices: a whole 4x4x8 slice. The times are simulated.
256 devices in a mesh: seq: 32 (over z, y), head: 8 (over x, core).
Axes of the slice: x: 4, y: 4, z: 8, core: 2. Of those that a mesh axis runs over, the one named last changes fastest.
Arguments:
- x_heads: bfloat16 [4096, 131072], P(('head', 'seq')), may hold values from -6 to 6
- b_proj: bfloat16 [131072, 128], P(('seq', 'head')), may hold values from -0.5 to 0.5
- c_proj: bfloat16 [131072, 128], P(('seq', 'head')), may hold values from -6 to 6
- log_gate: float32 [64, 131072], P('head', 'seq'), may hold values from -3 to 0, as said below
- step_size: float32 [64, 131072], P('head', 'seq'), may hold values from 0.003 to 0.03
- level_weight: float32 [64, 10, 131072], P('head', None, 'seq'), may hold values from 0.25 to 4
- skip: float32 [64], P('head'), may hold values from 0.5 to 1.5
Outputs:
- y_heads: bfloat16 [4096, 131072], P(('head', 'seq'))
Inputs may be any that keep to these rules, and one draw needn't show every extreme that they name: log_gate holds no positive values.
All inputs are finite; a program needn't handle non-finite values.
Results may differ from a plain program's by a relative error of at most 0.0064.
Values may be sent and summed in bfloat16 or wider, within the bound.
A program may use at most 192 MiB of HBM per device.

v0:
```python
import jax
import jax.numpy as jnp
import numpy as np
from jax import lax
from jax.sharding import PartitionSpec as P

P_SIZE = 64
N = 128
Q = 256


very_negative = -1e30


def on_device(x_heads, b_proj, c_proj, log_gate, step_size, level_weight, skip):
    head_count = log_gate.shape[0]
    tok_dev = log_gate.shape[1]
    span_count = tok_dev // Q
    state_width = N
    head_width = P_SIZE
    seq_count = lax.axis_size("seq")
    local_bits = span_count.bit_length() - 1
    shard_bits = seq_count.bit_length() - 1
    arranged = lax.all_to_all(x_heads, "seq", split_axis=1, concat_axis=0, tiled=True)
    values = arranged.reshape(head_count, head_width, span_count, Q)
    key_proj, query_proj = (
        lax.all_gather(b_proj, "head", axis=0, tiled=True),
        lax.all_gather(c_proj, "head", axis=0, tiled=True),
    )
    key_proj = key_proj.reshape(span_count, Q, state_width)
    query_proj = query_proj.reshape(span_count, Q, state_width)
    scores = jnp.einsum("cin,cjn->cij", query_proj, key_proj, preferred_element_type=jnp.float32)
    cumulative = jnp.cumsum(log_gate.reshape(head_count, span_count, Q), axis=2)
    step_blocks = step_size.reshape(head_count, span_count, Q)
    span_log = cumulative[:, :, -1]
    weighted = (
        values * (jnp.exp(span_log[:, :, None] - cumulative) * step_blocks)[:, None]
    ).astype(jnp.bfloat16)
    states = jnp.einsum("hpcj,cjn->chnp", weighted, key_proj, preferred_element_type=jnp.float32)
    starts = jnp.cumsum(span_log, axis=1) - span_log
    span_ids = np.arange(span_count)
    levels = []
    aggregate = states
    block_log = span_log.T
    for depth_bit in range(local_bits):
        blocks = span_ids >> depth_bit
        left_block = np.maximum(blocks - 1, 0)
        has_bit = (blocks & 1 == 1).astype(np.float32)
        decays = jnp.exp(starts[:, span_ids] - starts[:, blocks << depth_bit]).T * has_bit[:, None]
        levels.append((aggregate[left_block] * decays[:, :, None, None]).astype(jnp.bfloat16))
        pairs = aggregate.reshape(-1, 2, head_count, state_width, head_width)
        pair_logs = block_log.reshape(-1, 2, head_count)
        aggregate = jnp.exp(pair_logs[:, 1])[:, :, None, None] * pairs[:, 0] + pairs[:, 1]
        block_log = pair_logs[:, 0] + pair_logs[:, 1]
    summary = aggregate[0]
    total_log = block_log[0]
    shard_index = lax.axis_index("seq")
    shard_states = []
    every_state, every_log = (
        lax.all_gather(summary[None], "seq", axis=0, tiled=True),
        lax.all_gather(total_log[None], "seq", axis=0, tiled=True),
    )
    shard_ids = jnp.arange(seq_count)
    shard_ends = jnp.cumsum(every_log, axis=0)
    my_start = jnp.sum(
        jnp.where((shard_ids == shard_index)[:, None], shard_ends - every_log, 0.0), axis=0
    )
    for shard_bit in range(shard_bits):
        is_right = shard_index >> shard_bit & 1 == 1
        in_bucket = (shard_ids >> shard_bit == (shard_index >> shard_bit) - 1) & is_right
        gaps = jnp.where(in_bucket[:, None], my_start[None] - shard_ends, 0.0)
        weights = jnp.where(in_bucket[:, None], jnp.exp(gaps), 0.0)
        shard_states.append(
            jnp.einsum("ih,ihnp->hnp", weights, every_state, precision=lax.Precision.HIGHEST)
        )
    for shard_state in shard_states:
        levels.append(
            (shard_state[None] * jnp.exp(starts.T)[:, :, None, None]).astype(jnp.bfloat16)
        )
    stacked = jnp.stack(levels, axis=2)
    weight_blocks = level_weight.reshape(head_count, level_weight.shape[1], span_count, Q)
    token_positions = jnp.arange(Q)
    causal = token_positions[:, None] >= token_positions[None, :]

    def one_span(span_at, result):
        gate_tile = lax.dynamic_index_in_dim(cumulative, span_at, 1, keepdims=False)
        step_tile = lax.dynamic_index_in_dim(step_blocks, span_at, 1, keepdims=False)
        value_tile = lax.dynamic_index_in_dim(values, span_at, 2, keepdims=False)
        weight_tile = lax.dynamic_index_in_dim(weight_blocks, span_at, 2, keepdims=False)
        score_tile = lax.dynamic_index_in_dim(scores, span_at, 0, keepdims=False)
        query_tile = lax.dynamic_index_in_dim(query_proj, span_at, 0, keepdims=False)
        state_tile = lax.dynamic_index_in_dim(stacked, span_at, 0, keepdims=False)
        log_gaps = jnp.where(
            causal[None], gate_tile[:, :, None] - gate_tile[:, None, :], very_negative
        )
        mixing = (score_tile[None] * jnp.exp(log_gaps) * step_tile[:, None, :]).astype(jnp.bfloat16)
        local_part = jnp.einsum(
            "hij,hpj->hpi", mixing, value_tile, preferred_element_type=jnp.float32
        )
        local_part = local_part * weight_tile[:, 0, :][:, None, :]
        scaled = (weight_tile[:, 1:, :, None] * query_tile.astype(jnp.float32)[None, None]).astype(
            jnp.bfloat16
        )
        level_part = jnp.einsum(
            "hbin,hbnp->hpi", scaled, state_tile, preferred_element_type=jnp.float32
        )
        output_tile = (
            local_part
            + jnp.exp(gate_tile)[:, None, :] * level_part
            + skip[:, None, None] * value_tile.astype(jnp.float32)
        )
        return lax.dynamic_update_index_in_dim(result, output_tile.astype(jnp.bfloat16), span_at, 2)

    result = lax.fori_loop(
        0, span_count, one_span, jnp.zeros((head_count, head_width, span_count, Q), jnp.bfloat16)
    )
    merged = result.reshape(head_count * head_width, tok_dev)
    return lax.all_to_all(merged, "seq", split_axis=0, concat_axis=1, tiled=True)


def solution(mesh):
    in_specs = (
        P(("head", "seq"), None),
        P(("seq", "head"), None),
        P(("seq", "head"), None),
        P("head", "seq"),
        P("head", "seq"),
        P("head", None, "seq"),
        P("head"),
    )
    out_specs = P(("head", "seq"), None)
    return jax.shard_map(
        on_device, mesh=mesh, in_specs=in_specs, out_specs=out_specs, check_vma=False
    )
```

profile of v0, /device:TPU:32, one launch (start us, length us, event | category | flops | bytes accessed | tf_op | source)
XLA Modules:
  0.0 531.3 jit_solution(13705629255342241076)
XLA Ops:
  6.5 4.7 copy.227
  11.2 11.5 %all-to-all-start = ((bf16[16,32,4096]{2,0,1:T(8,128)(2,1)}), bf16[16,32,4096]{2,0,1:T(8,128)(2,1)}, u32[]{:S(2)}, u32[]{:S(2)}) async-start(bf16[16,32,4096]{2,0,1:T(8,128)(2,1)} %bitcast.224), calls=%async_computation | async-start | bytes 8388608 | tf_op jit(solution)/shard_map/all_to_all | solution.py:24
  24.4 4.6 reduce-window.6
  29.9 87.6 %all-to-all-done = bf16[16,32,4096]{2,0,1:T(8,128)(2,1)} async-done(((bf16[16,32,4096]{2,0,1:T(8,128)(2,1)}), bf16[16,32,4096]{2,0,1:T(8,128)(2,1)}, u32[]{:S(2)}, u32[]{:S(2)}) %all-to-all-start) | async-done | bytes 4194336 | tf_op jit(solution)/shard_map/all_to_all | solution.py:24
  117.5 3.6 copy.210
  121.1 2.0 copy-done.4
  123.1 3.0 multiply_convert_fusion.8
  126.0 4.0 fusion.26
  137.1 37.5 %all-gather = f32[32,1,8]{2,1,0:T(1,128)S(1)} all-gather(f32[1,1,8]{2,1,0:T(1,128)S(1)} %get-tuple-element.322), channel_id=2, replica_groups=mesh['seq'=32,'head'=8] {'seq'}, dimensions={0}, use_global_device_ids=true | all-gather | bytes 1056 | tf_op jit(solution)/shard_map/all_gather | solution.py:61
  174.8 2.8 copy.228
  177.9 4.2 fusion.47
  182.1 3.4 copy.162
  185.5 5.0 gather_fusion
  190.6 2.5 bitcast_add_fusion
  193.1 2.7 gather_fusion.2
  195.8 1.7 fusion.37
  197.6 2.9 gather_fusion.4
  200.6 2.8 gather_fusion.6
  203.4 4.2 fusion.33
  207.7 1.7 fusion.34
  210.7 1.8 fusion.35
  212.5 1.8 fusion.36
  214.2 14.5 %all-gather.9.cloned.1.call-done = f32[32,8,128,64]{2,3,1,0:T(8,128)} async-done(((f32[1,8,128,64]{2,3,1,0:T(8,128)}), f32[32,8,128,64]{2,3,1,0:T(8,128)}) %all-gather.9.cloned.1.call-update) | async-done | bytes 8388624 | tf_op jit(solution)/shard_map/all_gather | solution.py:60
  228.8 6.1 %multiply_reduce_fusion = (f32[8,128,64]{1,2,0:T(8,128)S(1)}, f32[8,128,64]{1,2,0:T(8,128)S(1)}, f32[8,128,64]{1,2,0:T(8,128)S(1)}, f32[8,128,64]{1,2,0:T(8,128)S(1)}, f32[8,128,64]{1,2,0:T(8,128)S(1)}) fusion(f32[32,8,128,64]{2,3,1,0:T(8,128)} %all-gather.9.cloned.1.call-done, f32[8,32]{0,1:T(8,128)S(1)} %get-tuple-element.311, ...), kind=kLoop, calls=%fused_computation.44 | loop fusion | flops 20643840 | bytes 9704448 | tf_op jit(solution)/shard_map/ih,ihnp->hnp/dot_general | solution.py:74
  234.9 1.8 fusion.28
  238.4 1.7 fusion.30
  241.9 1.7 fusion.32
  243.6 163.1 %while.14 = (s32[]{:T(128)}, bf16[8,64,16,256]{3,1,0,2:T(8,128)(2,1)}, bf16[8,64,16,256]{3,1,0,2:T(8,128)(2,1)}, f32[16,256,256]{2,1,0:T(8,128)}, f32[8,16,256]{...) while((s32[]{:T(128)}, ...), condition=%wide.region_6.7_spmd.clone, body=%wide.region_5.6_spmd.clone.sunk | while | flops 377454592 | bytes 5073025 | solution.py:114
  245.7 4.5 fusion.55
  251.3 2.5 fusion.56
  255.9 4.5 fusion.55
  261.5 2.5 fusion.56
  266.1 4.5 fusion.55
  271.7 2.5 fusion.56
  276.3 4.5 fusion.55
  281.9 2.5 fusion.56
  286.5 4.5 fusion.55
  292.1 2.5 fusion.56
  296.7 4.5 fusion.55
  302.3 2.5 fusion.56
  306.9 4.5 fusion.55
  312.5 2.5 fusion.56
  317.1 4.5 fusion.55
  322.7 2.5 fusion.56
  327.3 4.5 fusion.55
  332.9 2.5 fusion.56
  337.5 4.5 fusion.55
  343.1 2.5 fusion.56
  347.7 4.5 fusion.55
  353.3 2.5 fusion.56
  357.9 4.5 fusion.55
  363.5 2.5 fusion.56
  368.1 4.5 fusion.55
  373.7 2.5 fusion.56
  378.3 4.5 fusion.55
  383.8 2.5 fusion.56
  388.5 4.5 fusion.55
  394.0 2.5 fusion.56
  398.7 4.5 fusion.55
  404.2 2.5 fusion.56
  406.8 6.7 %copy.167 = bf16[8,64,16,256]{3,2,1,0:T(8,128)(2,1)} copy(bf16[8,64,16,256]{3,1,0,2:T(8,128)(2,1)} %get-tuple-element.189) | data formatting | bytes 8388608 | tf_op jit(solution)/shard_map/while | solution.py:114
  413.5 7.4 %all_to_all.29 = bf16[32,16,4096]{2,1,0:T(8,128)(2,1)} reshape(bf16[8,64,16,256]{3,2,1,0:T(8,128)(2,1)} %copy.167) | data formatting | bytes 8388608 | tf_op jit(solution)/shard_map/all_to_all | solution.py:118
  420.8 101.6 %all_to_all.35 = bf16[32,16,4096]{2,1,0:T(8,128)(2,1)S(1)} all-to-all(bf16[32,16,4096]{2,1,0:T(8,128)(2,1)} %all_to_all.29), channel_id=1, replica_groups=mesh['seq'=32,'head'=8] {'seq'}, dimensions={0} | all-to-all | bytes 8388608 | tf_op jit(solution)/shard_map/all_to_all | solution.py:118
  522.5 2.3 copy.209
  (255 shorter events, 63.8 us)
Async XLA Ops:
  11.2 13.1 %copy-start.9 = (f32[8,4096]{1,0:T(8,128)S(1)}, f32[8,4096]{1,0:T(8,128)}, u32[]{:S(2)}) copy-start(f32[8,4096]{1,0:T(8,128)} %param.37) | copy-start | bytes 393220
  11.2 18.5 %copy-start.8 = (f32[8,4096]{1,0:T(8,128)S(1)}, f32[8,4096]{1,0:T(8,128)}, u32[]{:S(2)}) copy-start(f32[8,4096]{1,0:T(8,128)} %param.38) | copy-start | bytes 393220
  11.2 106.2 %all-to-all-start = ((bf16[16,32,4096]{2,0,1:T(8,128)(2,1)}), bf16[16,32,4096]{2,0,1:T(8,128)(2,1)}, u32[]{:S(2)}, u32[]{:S(2)}) async-start(bf16[16,32,4096]{2,0,1:T(8,128)(2,1)} %bitcast.224), calls=%async_computation | async-start | bytes 8388608 | tf_op jit(solution)/shard_map/all_to_all | solution.py:24
  22.8 103.2 %all-gather.7.cloned.1.call-start = ((), (), s32[]{:S(2)}) async-start(), calls=%async_computation.3 | async-start | bytes 1179648 | tf_op jit(solution)/shard_map/all_gather | solution.py:27
  23.5 154.4 %all-gather.5.cloned.1.call-start = ((), (), s32[]{:S(2)}) async-start(), calls=%async_computation.2 | async-start | bytes 1179648 | tf_op jit(solution)/shard_map/all_gather | solution.py:28
  24.3 204.5 %all-gather.9.cloned.1.call-start = ((), (), s32[]{:S(2)}) async-start(), calls=%async_computation.4 | async-start | bytes 8650752 | tf_op jit(solution)/shard_map/all_gather | solution.py:60
  121.1 2.0 copy-start.4
  130.0 2.0 copy-start
  132.3 1.4 copy-start.6
  132.3 2.5 copy-start.19
  132.3 3.0 copy-start.18
  132.3 3.6 copy-start.16
  132.3 3.6 copy-start.17
  132.3 4.2 copy-start.14
  132.4 4.2 copy-start.15
  132.6 45.1 %copy-start.10 = (f32[16]{0:T(128)S(1)}, f32[16]{0:T(128)}, u32[]{:S(2)}) copy-start(f32[16]{0:T(128)} %constant.142) | copy-start | bytes 196
  132.6 45.1 %copy-start.11 = (f32[16]{0:T(128)S(1)}, f32[16]{0:T(128)}, u32[]{:S(2)}) copy-start(f32[16]{0:T(128)} %constant.145) | copy-start | bytes 196
  132.6 45.1 %copy-start.12 = (f32[16]{0:T(128)S(1)}, f32[16]{0:T(128)}, u32[]{:S(2)}) copy-start(f32[16]{0:T(128)} %constant.148) | copy-start | bytes 196
  132.6 45.1 %copy-start.13 = (f32[16]{0:T(128)S(1)}, f32[16]{0:T(128)}, u32[]{:S(2)}) copy-start(f32[16]{0:T(128)} %constant.150) | copy-start | bytes 196
  132.6 45.3 %copy-start.7 = (bf16[4096,128]{1,0:T(8,128)(2,1)S(1)}, bf16[4096,128]{1,0:T(8,128)(2,1)}, u32[]{:S(2)}) copy-start(bf16[4096,128]{1,0:T(8,128)(2,1)} %all-gather.7.cloned.1.call-done) | copy-start | bytes 3145732
  177.9 4.2 copy-start.5
  203.4 4.2 copy-start.1
  207.7 3.0 copy-start.2
  209.4 3.1 copy-start.3
  236.7 6.9 %copy-start.20 = (f32[8]{0:T(128)S(1)}, f32[8]{0:T(128)}, u32[]{:S(2)}) copy-start(f32[8]{0:T(128)} %param.40) | copy-start | bytes 100
Sparse Core Ops, SparseCore 0:
  25.5 26.7 all-gather.6
  54.1 25.6 all-gather.4
  134.6 94.0 all-gather.8
where the time goes:
time: 536 us; the launch traced here: 531 us
  blocking collectives  139 us (26%)
  matrix products  121 us (23%)
  waiting for transfers between devices  104 us (19%)
  local copies, waits for them, and re-layouts  88.7 us (17%)
  other arithmetic  52.6 us (10%)
  between operations  13.6 us (3%)
  starting transfers between devices  11.7 us (2%)
    all_to_all x1, blocking collectives, on_device(): lax.all_to_all(merged, 'seq', split_axis=0, concat_axis=1, tiled=True)  102 us
    all_to_all x1, waiting for transfers between devices, on_device(): lax.all_to_all(x_heads, 'seq', split_axis=1, concat_axis=0, tiled=True)  87.6 us
    dot_general x16, matrix products, one_span(): jnp.einsum('hbin,hbnp->hpi', scaled, state_tile, preferred_element_type=j...  72.4 us
    dot_general x16, matrix products, one_span(): jnp.einsum('hij,hpj->hpi', mixing, value_tile, preferred_element_type=jnp...  40.3 us
    all_gather x1, blocking collectives, on_device(): lax.all_gather(total_log[None], 'seq', axis=0, tiled=True)  37.5 us
    dynamic_slice x32, local copies, waits for them, and re-layouts, one_span(): lax.dynamic_index_in_dim(weight_blocks, span_at, 2, keepdims=False)  18.5 us
    unnamed x9, other arithmetic  16.6 us
    mul x16, local copies, waits for them, and re-layouts, one_span(): score_tile[None] * jnp.exp(log_gaps) * step_tile[:, None, :]  15.6 us
  transfers between devices with their start and end apart: 4, of which 2 were waited for; matrix products, arithmetic and copies ran while one was open for 11% of the time, Pallas kernels for 0%

commit v1 on v0

v1 whole, which is shorter than its diff:
```python
import functools

import jax
import jax.numpy as jnp
import numpy as np
from jax import lax
from jax.experimental import pallas as pl
from jax.experimental.pallas import tpu as pltpu
from jax.sharding import Mesh, PartitionSpec as P

P_SIZE = 64
N = 128
Q = 256
LO = 4
SPANS = 1 << LO
SHARD = SPANS * Q
LOG2E = 1.4426950408889634
NT = (((1,), (1,)), ((), ()))
F32 = jnp.float32
BF16 = jnp.bfloat16


def dot(a, b):
    return jnp.dot(a, b, preferred_element_type=F32)


def dot_nt(a, b):
    return lax.dot_general(a, b, NT, preferred_element_type=F32)


def span_cols(k):
    return pl.ds(pl.multiple_of(k * Q, Q), Q)


def states_body(lev, x_ref, b_ref, gp_ref, slow_ref, rows_ref, sum_ref, tot_ref, g_scr, st_scr):
    for k in range(SPANS):
        piece = gp_ref[0, lev : lev + 6, k * Q : (k + 1) * Q].astype(F32)
        for m in range(3):
            g_scr[m, k : k + 1, :] = piece[m : m + 1]
        g_scr[3, k : k + 1, :] = piece[3:4] + piece[4:5] + piece[5:6]
    upper = (
        lax.broadcasted_iota(jnp.int32, (Q, Q), 0) <= lax.broadcasted_iota(jnp.int32, (Q, Q), 1)
    ).astype(BF16)
    cum = dot(g_scr[0].astype(BF16), upper)
    cum = cum + dot(g_scr[1].astype(BF16), upper)
    cum = (cum + dot(g_scr[2].astype(BF16), upper)) * LOG2E
    step = g_scr[3]
    decay = jnp.exp2(cum[:, Q - 1 :] - cum) * step
    g_scr[0] = decay
    for k in range(SPANS):
        rows_ref[0, k, 0:1, :] = cum[k : k + 1]
        rows_ref[0, k, 1:2, :] = step[k : k + 1]
    logs = [jnp.broadcast_to(cum[k : k + 1, Q - 1 :], (1, N)) for k in range(SPANS)]
    starts = [jnp.zeros((1, N), F32)]
    for k in range(SPANS):
        starts.append(starts[-1] + logs[k])
    for k in range(SPANS):
        rows_ref[0, k, 2:3, :] = jnp.concatenate([starts[k], starts[k]], axis=1)

    def one(k, carry):
        cols = span_cols(k)
        w = x_ref[:, cols].astype(F32) * g_scr[0, pl.ds(k, 1), :]
        st_scr[k] = dot(w.astype(BF16), b_ref[pl.ds(pl.multiple_of(k * Q, Q), Q), :])
        return carry

    lax.fori_loop(0, SPANS, one, 0)
    agg = [st_scr[k] for k in range(SPANS)]
    block_logs = list(logs)
    for bit in range(LO):
        for k in range(SPANS):
            if (k >> bit) & 1:
                left = agg[(k >> bit) - 1]
                scale = jnp.exp2(starts[k] - starts[(k >> bit) << bit])
                slow_ref[0, k, bit * P_SIZE : (bit + 1) * P_SIZE, :] = (left * scale).astype(BF16)
            else:
                slow_ref[0, k, bit * P_SIZE : (bit + 1) * P_SIZE, :] = jnp.zeros((P_SIZE, N), BF16)
        agg = [
            jnp.exp2(block_logs[2 * m + 1]) * agg[2 * m] + agg[2 * m + 1]
            for m in range(len(agg) // 2)
        ]
        block_logs = [block_logs[2 * m] + block_logs[2 * m + 1] for m in range(len(block_logs) // 2)]
    sum_ref[0] = agg[0]
    tot_ref[0] = jnp.broadcast_to(block_logs[0], (8, N))


def main_body(lev, x_ref, b_ref, c_ref, gp_ref, slow_ref, shi_ref, rows_ref, skip_ref, out_ref):
    hi = lev - 1 - LO
    half = Q // 2
    tri = lax.broadcasted_iota(jnp.int32, (half, half), 0) <= lax.broadcasted_iota(
        jnp.int32, (half, half), 1
    )
    skip = skip_ref[0:1, 0:1]

    def one(k, carry):
        cols = span_cols(k)
        toks = pl.ds(pl.multiple_of(k * Q, Q), Q)
        x = x_ref[:, cols].astype(F32)
        b = b_ref[toks, :]
        c = c_ref[toks, :]
        tile = rows_ref[0, k]
        cum = tile[0:1, :]
        cum_col = jnp.transpose(tile)[:, 0:1]
        xs = (x * tile[1:2, :]).astype(BF16)
        top = dot_nt(b[:half], c) * jnp.exp2(cum - cum_col[:half])
        low = dot_nt(b[half:], c[half:]) * jnp.exp2(cum[:, half:] - cum_col[half:])
        m00 = jnp.where(tri, top[:, :half], 0.0).astype(BF16)
        m01 = top[:, half:].astype(BF16)
        m11 = jnp.where(tri, low, 0.0).astype(BF16)
        left = dot(xs[:, :half], m00)
        right = dot(xs, jnp.concatenate([m01, m11], axis=0))
        local = jnp.concatenate([left, right], axis=1)
        lw = gp_ref[0, :, cols].astype(F32)
        r_lo = dot_nt(slow_ref[0, k], c)
        r_hi = dot_nt(shi_ref[0], c)
        e_lo = jnp.exp2(cum)
        e_hi = jnp.exp2(cum + tile[2:3, :])
        acc = local * lw[0:1] + skip * x
        for bit in range(LO):
            acc = acc + r_lo[bit * P_SIZE : (bit + 1) * P_SIZE] * (lw[1 + bit : 2 + bit] * e_lo)
        for bit in range(hi):
            at = 1 + LO + bit
            acc = acc + r_hi[bit * P_SIZE : (bit + 1) * P_SIZE] * (lw[at : at + 1] * e_hi)
        out_ref[:, cols] = acc.astype(BF16)
        return carry

    lax.fori_loop(0, SPANS, one, 0)


def pieces(v):
    first = lax.reduce_precision(v, 8, 7)
    rest = v - first
    second = lax.reduce_precision(rest, 8, 7)
    return [first, second, rest - second]


def on_device(x_heads, b_proj, c_proj, log_gate, step_size, level_weight, skip):
    nz = lax.axis_size("z")
    ny = lax.axis_size("y")
    y_at = lax.axis_index("y")
    z_at = lax.axis_index("z")
    rows = x_heads.shape[0]
    lev = level_weight.shape[1]
    hi = lev - 1 - LO
    tok = nz * SHARD

    parts = [level_weight[:, i] for i in range(lev)] + pieces(log_gate) + pieces(step_size)
    parts += [jnp.zeros_like(log_gate)] * (16 - len(parts))
    packed = jnp.stack(parts, axis=1).astype(BF16)
    gates = lax.all_to_all(packed, "z", split_axis=0, concat_axis=0, tiled=True)
    x = x_heads.reshape(rows, nz, ny, SHARD)
    x = lax.all_to_all(x, "y", split_axis=2, concat_axis=0, tiled=True).reshape(ny * rows, tok)
    b = lax.all_gather(b_proj, ("z", "x", "core"), axis=0, tiled=True)
    c = lax.all_gather(c_proj, ("z", "x", "core"), axis=0, tiled=True)
    my_skip = jnp.broadcast_to(lax.dynamic_slice(skip, (z_at,), (1,))[:, None], (8, 128))

    x_spec = pl.BlockSpec((P_SIZE, SHARD), lambda i: (0, i))
    t_spec = pl.BlockSpec((SHARD, N), lambda i: (i, 0))
    g_spec = pl.BlockSpec((1, 16, SHARD), lambda i: (i, 0, 0))
    slow_spec = pl.BlockSpec((1, SPANS, LO * P_SIZE, N), lambda i: (i, 0, 0, 0))
    rows_spec = pl.BlockSpec((1, SPANS, 8, Q), lambda i: (i, 0, 0, 0))
    params = pltpu.CompilerParams(vmem_limit_bytes=48 << 20)
    slow, tiles, summary, total = pl.pallas_call(
        functools.partial(states_body, lev),
        grid=(nz,),
        in_specs=[x_spec, t_spec, g_spec],
        out_specs=[
            slow_spec,
            rows_spec,
            pl.BlockSpec((1, P_SIZE, N), lambda i: (i, 0, 0)),
            pl.BlockSpec((1, 8, N), lambda i: (i, 0, 0)),
        ],
        out_shape=[
            jax.ShapeDtypeStruct((nz, SPANS, LO * P_SIZE, N), BF16),
            jax.ShapeDtypeStruct((nz, SPANS, 8, Q), F32),
            jax.ShapeDtypeStruct((nz, P_SIZE, N), F32),
            jax.ShapeDtypeStruct((nz, 8, N), F32),
        ],
        scratch_shapes=[pltpu.VMEM((4, SPANS, Q), F32), pltpu.VMEM((SPANS, P_SIZE, N), F32)],
        compiler_params=params,
        name="states",
    )(x, b, gates)

    every = lax.all_gather(summary, "y", axis=1)
    logs = lax.all_gather(total[:, 0, 0], "y", axis=1).reshape(nz * ny)
    ends = jnp.cumsum(logs)
    ids = jnp.arange(nz * ny)
    mine = jnp.arange(nz) * ny + y_at
    start = jnp.sum(jnp.where(ids[None] == mine[:, None], (ends - logs)[None], 0.0), axis=1)
    bits = jnp.arange(hi)
    own = mine[:, None] >> bits[None]
    inside = (ids[None, None] >> bits[None, :, None] == own[:, :, None] - 1) & (
        (own & 1) == 1
    )[:, :, None]
    gap = jnp.where(inside, start[:, None, None] - ends[None, None], 0.0)
    weights = jnp.where(inside, jnp.exp2(gap), 0.0)
    shi = jnp.einsum(
        "zks,spn->zkpn",
        weights,
        every.reshape(nz * ny, P_SIZE, N),
        precision=lax.Precision.HIGHEST,
    )
    shi = shi.astype(BF16).reshape(nz, hi * P_SIZE, N)

    out = pl.pallas_call(
        functools.partial(main_body, lev),
        grid=(nz,),
        in_specs=[
            x_spec,
            t_spec,
            t_spec,
            g_spec,
            slow_spec,
            pl.BlockSpec((1, hi * P_SIZE, N), lambda i: (i, 0, 0)),
            rows_spec,
            pl.BlockSpec((8, 128), lambda i: (0, 0)),
        ],
        out_specs=x_spec,
        out_shape=jax.ShapeDtypeStruct((P_SIZE, tok), BF16),
        compiler_params=params,
        name="outputs",
    )(x, b, c, gates, slow, shi, tiles, my_skip)

    out = out.reshape(ny * rows, nz, 1, SHARD)
    out = lax.all_to_all(out, "y", split_axis=0, concat_axis=2, tiled=True)
    return out.reshape(rows, nz * ny * SHARD)


def build(mesh):
    group = ("x", "core")
    seq = ("z", "y")
    in_specs = (
        P(group + seq, None),
        P(seq + group, None),
        P(seq + group, None),
        P(group, seq),
        P(group, seq),
        P(group, None, seq),
        P(group),
    )
    return jax.shard_map(
        on_device, mesh=mesh, in_specs=in_specs, out_specs=P(group + seq, None), check_vma=False
    )


def solution(mesh):
    shape = (8, 4, 4, 2)
    return build(Mesh(mesh.devices.reshape(shape), ("z", "y", "x", "core")))
```

time: 536 us -> 393 us (0.73)
  matrix products: 121 us -> 3.01 us
  Pallas kernels: 0 us -> 91 us
  blocking collectives: 139 us -> 62.3 us
  waiting for transfers between devices: 104 us -> 162 us
  other arithmetic: 52.6 us -> 0.58 us
  local copies, waits for them, and re-layouts: 88.7 us -> 45.3 us
    dot_general x34 -> x1, matrix products: 121 us -> 3.01 us  [on_device(): jnp.einsum('zks,spn->zkpn', weights, every.reshape(nz * ny, P_SIZE, N), p...]
    pallas_call x0 -> x2, Pallas kernels: none -> 91 us  [the longest x1 67.5 us: on_device(): pl.pallas_call(functools.partial(main_body, lev), grid=(nz,), in_specs=[x...]
    all_gather x3, waiting for transfers between devices: 14.5 us -> 94.7 us  [the longest x1 82.6 us: on_device(): c = lax.all_gather(c_proj, ('z', 'x', 'core'), axis=0, tiled=True)]
    all_to_all x1, blocking collectives: 102 us -> 53.3 us  [on_device(): out = lax.all_to_all(out, 'y', split_axis=0, concat_axis=2, tiled=True)]
    all_gather x1, blocking collectives: 37.5 us -> 8.99 us  [on_device(): logs = lax.all_gather(total[:, 0, 0], 'y', axis=1).reshape(nz * ny)]
    all_to_all x1 -> x2, waiting for transfers between devices: 87.6 us -> 66.1 us  [the longest x1 41.5 us: on_device(): lax.all_to_all(x, 'y', split_axis=2, concat_axis=0, tiled=True)]
    reshape x1 -> x4, local copies, waits for them, and re-layouts: 0.05 us -> 19.3 us  [the longest x2 13.2 us: on_device(): x = x_heads.reshape(rows, nz, ny, SHARD)]
    dynamic_slice x48 -> x1, local copies, waits for them, and re-layouts: 18.7 us -> 0.67 us  [on_device(): lax.dynamic_slice(skip, (z_at,), (1,))[:, None]]
  transfers between devices with their start and end apart: 4 -> 5, of which waited for: 2 -> 4; matrix products, arithmetic and copies ran while one was open for 11% -> 8% of each run, Pallas kernels for 0% -> 0%
where the time goes in v1:
time: 393 us; the launch traced here: 391 us
  waiting for transfers between devices  162 us (41%)
  Pallas kernels  91 us (23%)
  blocking collectives  62.3 us (16%)
  local copies, waits for them, and re-layouts  45.3 us (12%)
  starting transfers between devices  13.7 us (3%)
  between operations  13.3 us (3%)
    all_gather x1, waiting for transfers between devices, on_device(): c = lax.all_gather(c_proj, ('z', 'x', 'core'), axis=0, tiled=True)  82.6 us
    pallas_call x1, Pallas kernels, on_device(): pl.pallas_call(functools.partial(main_body, lev), grid=(nz,), in_specs=[x...  67.5 us
    all_to_all x1, blocking collectives, on_device(): out = lax.all_to_all(out, 'y', split_axis=0, concat_axis=2, tiled=True)  53.3 us
    all_to_all x1, waiting for transfers between devices, on_device(): lax.all_to_all(x, 'y', split_axis=2, concat_axis=0, tiled=True)  41.5 us
    all_to_all x1, waiting for transfers between devices, on_device(): gates = lax.all_to_all(packed, 'z', split_axis=0, concat_axis=0, tiled=True)  24.7 us
    pallas_call x1, Pallas kernels, on_device(): pl.pallas_call(functools.partial(states_body, lev), grid=(nz,), in_specs=...  23.5 us
    reshape x2, local copies, waits for them, and re-layouts, on_device(): x = x_heads.reshape(rows, nz, ny, SHARD)  13.2 us
    all_gather x1, waiting for transfers between devices, on_device(): every = lax.all_gather(summary, 'y', axis=1)  12.1 us
  transfers between devices with their start and end apart: 5, of which 4 were waited for; matrix products, arithmetic and copies ran while one was open for 8% of the time, Pallas kernels for 0%

profile of v1, /device:TPU:32, one launch (start us, length us, event | category | flops | bytes accessed | tf_op | source)
XLA Modules:
  0.0 391.5 jit_solution(12541329465773958292)
XLA Ops:
  6.5 0.0 all-gather.6.cloned.1.call-start
  6.5 0.7 all-gather.6.cloned.1.call-update
  7.3 6.8 %reshape.144 = bf16[16,8,4,4096]{3,2,1,0:T(4,128)(2,1)} reshape(bf16[16,131072]{1,0:T(8,128)(2,1)} %param.7) | data formatting | bytes 8388608 | tf_op jit(solution)/shard_map/reshape | solution.py:150
  14.1 6.4 %copy.82 = bf16[16,8,4,4096]{3,1,0,2:T(8,128)(2,1)} copy(bf16[16,8,4,4096]{3,2,1,0:T(4,128)(2,1)} %reshape.144) | data formatting | bytes 8388608 | tf_op jit(solution)/shard_map/reshape | solution.py:150
  20.5 0.0 copy-start.1
  20.5 0.0 copy-start.2
  20.5 0.0 copy-start
  20.5 5.1 %all-to-all-start = ((bf16[16,8,4,4096]{3,1,0,2:T(8,128)(2,1)}), bf16[16,8,4,4096]{3,1,0,2:T(8,128)(2,1)}, u32[]{:S(2)}, u32[]{:S(2)}) async-start(bf16[16,8,4,4096]{3,1,0,2:T(8,128)(2,1)} %copy.82), calls=%async_computation | async-start | bytes 8388608 | tf_op jit(solution)/shard_map/all_to_all | solution.py:151
  25.6 0.0 copy-done.1
  25.6 0.1 copy.86
  25.7 0.1 copy.85
  25.8 0.1 copy.84
  25.9 0.0 copy-done.2
  26.0 0.1 copy.89
  26.1 0.1 copy.88
  26.2 0.1 copy.87
  26.3 0.0 copy-done
  26.3 0.1 convert.27
  26.4 0.4 copy.83
  26.8 6.5 %stack.35 = bf16[8,16,4096]{2,1,0:T(8,128)(2,1)} concatenate(bf16[8,10,4096]{2,1,0:T(8,128)(2,1)S(1)} %copy.83, bf16[8,1,4096]{2,1,0:T(2,128)(2,1)S(1)} %copy.84, bf16[8,1,4096]{2,1,0:T(2,128)(2,1)S(1)} %copy.85, bf16[8,1,4096]{2,1,0:T(2,128)(2,1)S(1)} %copy.86, bf16[8,1,4096]{2,1,0:T(2,128)(2,1)S(1)} %copy.87, bf16[8,1,4096]{2,1,0:T(2,128)(2,1)S(1)} %copy.88, ...), dimensions={1} | concatenate | bytes 2097152 | tf_op jit(solution)/shard_map/stack | solution.py:148
  33.2 41.5 %all-to-all-done = bf16[16,8,4,4096]{3,1,0,2:T(8,128)(2,1)} async-done(((bf16[16,8,4,4096]{3,1,0,2:T(8,128)(2,1)}), bf16[16,8,4,4096]{3,1,0,2:T(8,128)(2,1)}, u32[]{:S(2)}, u32[]{:S(2)}) %all-to-all-start) | async-done | bytes 4194336 | tf_op jit(solution)/shard_map/all_to_all | solution.py:151
  74.7 8.6 %all-to-all-start.1 = ((bf16[8,16,4096]{2,1,0:T(8,128)(2,1)}), bf16[8,16,4096]{2,1,0:T(8,128)(2,1)S(1)}, u32[]{:S(2)}, u32[]{:S(2)}) async-start(bf16[8,16,4096]{2,1,0:T(8,128)(2,1)} %stack.35), calls=%async_computation.1 | async-start | bytes 2097152 | tf_op jit(solution)/shard_map/all_to_all | solution.py:149
  83.3 0.0 all-gather.10.cloned.1.call-start
  83.3 6.9 %copy.99 = bf16[8,8,8,4096]{3,1,2,0:T(8,128)(2,1)} copy(bf16[8,8,8,4096]{3,2,1,0:T(8,128)(2,1)} %bitcast.22) | data formatting | bytes 8388608
  90.1 24.7 %all-to-all-done.1.gp_ref = bf16[8,16,4096]{2,1,0:T(8,128)(2,1)S(1)} async-done(((bf16[8,16,4096]{2,1,0:T(8,128)(2,1)}), bf16[8,16,4096]{2,1,0:T(8,128)(2,1)S(1)}, u32[]{:S(2)}, u32[]{:S(2)}) %all-to-all-start.1) | async-done | bytes 1048608 | tf_op jit(solution)/shard_map/all_to_all | solution.py:149
  114.8 0.0 all-gather.6.cloned.1.call-done.b_ref
  114.8 0.0 copy-start.3
  114.8 23.5 %states.1 = (bf16[8,16,256,128]{3,2,1,0:T(8,128)(2,1)}, f32[8,16,8,256]{3,2,1,0:T(8,128)S(1)}, f32[8,64,128]{2,1,0:T(8,128)}, f32[8,8,128]{2,1,0:T(8,128)S(1)}) custom-call(bf16[64,32768]{1,0:T(8,128)(2,1)} %bitcast.46, bf16[32768,128]{1,0:T(8,128)(2,1)} %all-gather.6.cloned.1.call-done.b_ref, bf16[8,16,4096]{2,1,0:T(8,128)(2,1)S(1)} %all-to-all-done.1.gp_ref), custom_call_target="tpu_custom_call" | custom-call | tf_op jit(solution)/shard_map/states/pallas_call | solution.py:162
  138.3 0.0 all-gather.10.cloned.1.call-update
  138.3 0.0 all-gather.8.cloned.1.call-start
  138.4 0.7 all-gather.8.cloned.1.call-update
  139.1 0.1 copy.90
  139.2 0.0 copy-done.3
  139.2 0.7 dynamic_slice.3
  139.9 9.0 %all-gather = f32[8,4,1]{0,2,1:T(1,128)S(1)} all-gather(f32[8,1,1]{0,2,1:T(1,128)S(1)} %copy.90), channel_id=2, replica_groups=mesh['z'=8,'y'=4,'x'=4,'core'=2] {'y'}, dimensions={1}, use_global_device_ids=true | all-gather | bytes 160 | tf_op jit(solution)/shard_map/all_gather | solution.py:184
  148.9 0.1 copy.91
  149.0 0.1 reshape.148
  149.1 0.1 reshape.160
  149.1 0.1 reduce-window.7
  149.2 0.1 reduce
  149.3 0.2 select_reduce_fusion
  149.5 0.1 broadcast_subtract_fusion
  149.6 12.1 %all-gather.10.cloned.1.call-done = f32[8,256,128]{2,1,0:T(8,128)} async-done(((f32[8,64,128]{2,1,0:T(8,128)}), f32[8,256,128]{2,1,0:T(8,128)}) %all-gather.10.cloned.1.call-update) | async-done | bytes 1048592 | tf_op jit(solution)/shard_map/all_gather | solution.py:183
  161.7 3.0 convolution_convert_fusion
  164.7 0.1 copy.95
  164.9 82.6 %all-gather.8.cloned.1.call-done.c_ref = bf16[32768,128]{1,0:T(8,128)(2,1)} async-done(((bf16[512,128]{1,0:T(8,128)(2,1)}), bf16[32768,128]{1,0:T(8,128)(2,1)}) %all-gather.8.cloned.1.call-update) | async-done | bytes 8388624 | tf_op jit(solution)/shard_map/all_gather | solution.py:153
  247.4 0.7 broadcast_in_dim.50.skip_ref
  248.1 67.5 %outputs.1 = bf16[64,32768]{1,0:T(8,128)(2,1)} custom-call(bf16[64,32768]{1,0:T(8,128)(2,1)} %bitcast.47, bf16[32768,128]{1,0:T(8,128)(2,1)} %all-gather.6.cloned.1.call-done.b_ref, bf16[32768,128]{1,0:T(8,128)(2,1)} %all-gather.8.cloned.1.call-done.c_ref, bf16[8,16,4096]{2,1,0:T(8,128)(2,1)S(1)} %all-to-all-done.1.gp_ref, ...), custom_call_target="tpu_custom_call" | custom-call | tf_op jit(solution)/shard_map/outputs/pallas_call | solution.py:204
  315.7 4.5 %copy.100 = bf16[8,8,8,4096]{3,2,1,0:T(8,128)(2,1)S(1)} copy(bf16[8,8,8,4096]{3,1,2,0:T(8,128)(2,1)} %bitcast.48) | data formatting | bytes 8388608
  320.2 53.3 %all_to_all.35 = bf16[64,8,1,4096]{3,1,2,0:T(8,128)(2,1)S(1)} all-to-all(bf16[64,8,1,4096]{3,1,2,0:T(8,128)(2,1)S(1)} %bitcast.49), channel_id=1, replica_groups=mesh['z'=8,'y'=4,'x'=4,'core'=2] {'y'}, dimensions={0} | all-to-all | bytes 8388608 | tf_op jit(solution)/shard_map/all_to_all | solution.py:224
  373.5 5.5 %copy.97 = bf16[16,8,4,1,4096]{4,2,1,0,3:T(4,128)(2,1)} copy(bf16[16,8,4,1,4096]{4,1,0,2,3:T(8,128)(2,1)S(1)} %bitcast.50) | data formatting | bytes 8388608 | tf_op jit(solution)/shard_map/all_to_all | solution.py:224
  379.0 6.0 %reshape.152 = bf16[16,131072]{1,0:T(8,128)(2,1)} reshape(bf16[16,8,4,1,4096]{4,2,1,0,3:T(4,128)(2,1)} %copy.97) | data formatting | bytes 8388608 | tf_op jit(solution)/shard_map/reshape | solution.py:225
  (8 shorter events, 0.1 us)
Async XLA Ops:
  6.5 108.3 %all-gather.6.cloned.1.call-start = ((), (), s32[]{:S(2)}) async-start(), calls=%async_computation.3 | async-start | bytes 8519680 | tf_op jit(solution)/shard_map/all_gather | solution.py:152
  20.5 5.1 %copy-start.1 = (f32[8,4096]{1,0:T(8,128)S(1)}, f32[8,4096]{1,0:T(8,128)}, u32[]{:S(2)}) copy-start(f32[8,4096]{1,0:T(8,128)} %param.10) | copy-start | bytes 393220
  20.5 5.5 %copy-start.2 = (f32[8,4096]{1,0:T(8,128)S(1)}, f32[8,4096]{1,0:T(8,128)}, u32[]{:S(2)}) copy-start(f32[8,4096]{1,0:T(8,128)} %param.11) | copy-start | bytes 393220
  20.5 5.8 %copy-start = (f32[8,10,4096]{2,0,1:T(8,128)S(1)}, f32[8,10,4096]{2,0,1:T(8,128)}, u32[]{:S(2)}) copy-start(f32[8,10,4096]{2,0,1:T(8,128)} %param.12) | copy-start | bytes 3932164
  20.5 54.2 %all-to-all-start = ((bf16[16,8,4,4096]{3,1,0,2:T(8,128)(2,1)}), bf16[16,8,4,4096]{3,1,0,2:T(8,128)(2,1)}, u32[]{:S(2)}, u32[]{:S(2)}) async-start(bf16[16,8,4,4096]{3,1,0,2:T(8,128)(2,1)} %copy.82), calls=%async_computation | async-start | bytes 8388608 | tf_op jit(solution)/shard_map/all_to_all | solution.py:151
  74.7 40.1 %all-to-all-start.1 = ((bf16[8,16,4096]{2,1,0:T(8,128)(2,1)}), bf16[8,16,4096]{2,1,0:T(8,128)(2,1)S(1)}, u32[]{:S(2)}, u32[]{:S(2)}) async-start(bf16[8,16,4096]{2,1,0:T(8,128)(2,1)} %stack.35), calls=%async_computation.1 | async-start | bytes 2097152 | tf_op jit(solution)/shard_map/all_to_all | solution.py:149
  83.3 78.4 %all-gather.10.cloned.1.call-start = ((), (), s32[]{:S(2)}) async-start(), calls=%async_computation.5 | async-start | bytes 1310720 | tf_op jit(solution)/shard_map/all_gather | solution.py:183
  114.8 24.4 %copy-start.3 = (f32[8]{0:T(128)S(1)}, f32[8]{0:T(128)}, u32[]{:S(2)}) copy-start(f32[8]{0:T(128)} %param.13) | copy-start | bytes 100
  138.3 109.1 %all-gather.8.cloned.1.call-start = ((), (), s32[]{:S(2)}) async-start(), calls=%async_computation.4 | async-start | bytes 8519680 | tf_op jit(solution)/shard_map/all_gather | solution.py:153
Sparse Core Ops, SparseCore 0:
  10.1 97.7 all-gather.5
  138.5 23.2 all-gather.9
  164.5 82.9 all-gather.7

commit v2 on v1

v2 whole, which is shorter than its diff:
```python
import functools

import jax
import jax.numpy as jnp
from jax import lax
from jax.experimental import pallas as pl
from jax.experimental.pallas import tpu as pltpu
from jax.sharding import Mesh, PartitionSpec as P

P_SIZE = 64
N = 128
Q = 256
LO = 4
SPANS = 1 << LO
SHARD = SPANS * Q
LOG2E = 1.4426950408889634
NT = (((1,), (1,)), ((), ()))
F32 = jnp.float32
BF16 = jnp.bfloat16
MESH = pl.DeviceIdType.MESH
AXES = ("z", "y", "x", "core")


def dot(a, b):
    return jnp.dot(a, b, preferred_element_type=F32)


def dot_nt(a, b):
    return lax.dot_general(a, b, NT, preferred_element_type=F32)


def span_at(k):
    return pl.ds(pl.multiple_of(k * Q, Q), Q)


def pack_gates(lev, h, lw_ref, lg_ref, st_ref, tmp, pk):
    tmp[0:lev, :] = lw_ref[h]
    for row, ref in ((lev, lg_ref), (lev + 3, st_ref)):
        v = ref[pl.ds(h, 1), :]
        first = v.astype(BF16).astype(F32)
        rest = v - first
        second = rest.astype(BF16).astype(F32)
        tmp[row : row + 1, :] = first
        tmp[row + 1 : row + 2, :] = second
        tmp[row + 2 : row + 3, :] = rest - second
    pk[h] = tmp[...].astype(BF16)


def shard_states(lev, r, xb, bb, gb, slow, tiles, g_scr, st_scr):
    for k in range(SPANS):
        piece = gb[r, :, k * Q : (k + 1) * Q].astype(F32)
        for m in range(3):
            g_scr[m, k : k + 1, :] = piece[lev + m : lev + m + 1]
        g_scr[3, k : k + 1, :] = (
            piece[lev + 3 : lev + 4] + piece[lev + 4 : lev + 5] + piece[lev + 5 : lev + 6]
        )
    upper = (
        lax.broadcasted_iota(jnp.int32, (Q, Q), 0) <= lax.broadcasted_iota(jnp.int32, (Q, Q), 1)
    ).astype(BF16)
    cum = dot(g_scr[0].astype(BF16), upper)
    cum = cum + dot(g_scr[1].astype(BF16), upper)
    cum = (cum + dot(g_scr[2].astype(BF16), upper)) * LOG2E
    step = g_scr[3]
    g_scr[0] = jnp.exp2(cum[:, Q - 1 :] - cum) * step
    logs = [jnp.broadcast_to(cum[k : k + 1, Q - 1 :], (1, N)) for k in range(SPANS)]
    starts = [jnp.zeros((1, N), F32)]
    for k in range(SPANS):
        starts.append(starts[-1] + logs[k])
    for k in range(SPANS):
        tiles[r, k, 0:1, :] = cum[k : k + 1]
        tiles[r, k, 1:2, :] = step[k : k + 1]
        tiles[r, k, 2:3, :] = jnp.concatenate([starts[k], starts[k]], axis=1)

    def one(k, carry):
        w = xb[r, :, span_at(k)].astype(F32) * g_scr[0, pl.ds(k, 1), :]
        st_scr[k] = dot(w.astype(BF16), bb[r, span_at(k), :])
        return carry

    lax.fori_loop(0, SPANS, one, 0, unroll=2)
    agg = [st_scr[k] for k in range(SPANS)]
    block_logs = list(logs)
    for bit in range(LO):
        rows = slice(bit * P_SIZE, (bit + 1) * P_SIZE)
        for k in range(SPANS):
            if (k >> bit) & 1:
                scale = jnp.exp2(starts[k] - starts[(k >> bit) << bit])
                slow[r, k, rows, :] = (agg[(k >> bit) - 1] * scale).astype(BF16)
            else:
                slow[r, k, rows, :] = jnp.zeros((P_SIZE, N), BF16)
        pairs = range(len(agg) // 2)
        agg = [jnp.exp2(block_logs[2 * m + 1]) * agg[2 * m] + agg[2 * m + 1] for m in pairs]
        block_logs = [block_logs[2 * m] + block_logs[2 * m + 1] for m in pairs]
    return agg[0], block_logs[0]


def shard_levels(nz, ny, z, y, sums, shi):
    ybits = ny.bit_length() - 1
    zbits = nz.bit_length() - 1
    slots = [lax.rem(zz - z + nz, nz) for zz in range(nz)]
    before = [jnp.where(yy < y, 1.0, 0.0) for yy in range(ny)]
    belongs = []
    for b in range(ybits):
        own = y // (1 << b)
        odd = lax.rem(own, 2) == 1
        belongs.append(
            [jnp.where(odd & (own - 1 == yy >> b), 1.0, 0.0) for yy in range(ny)]
        )
    agg, totals, lead = [], [], []
    for zz in range(nz):
        logs = [sums[yy, slots[zz], P_SIZE : P_SIZE + 1, :] for yy in range(ny)]
        ahead = logs[0] * before[0]
        for yy in range(1, ny):
            ahead = ahead + logs[yy] * before[yy]
        lead.append(ahead)
        after = jnp.zeros((1, N), F32)
        near = jnp.zeros((1, N), F32)
        whole = None
        parts = [None] * ybits
        for yy in reversed(range(ny)):
            state = sums[yy, slots[zz], 0:P_SIZE, :]
            term = state * jnp.exp2(after)
            whole = term if whole is None else whole + term
            scale = jnp.exp2(near)
            for b in range(ybits):
                term = state * (scale * belongs[b][yy])
                parts[b] = term if parts[b] is None else parts[b] + term
            after = after + logs[yy]
            near = near + logs[yy] * before[yy]
        agg.append(whole)
        totals.append(after)
        for b in range(ybits):
            shi[slots[zz], b * P_SIZE : (b + 1) * P_SIZE, :] = parts[b].astype(BF16)
    starts = [jnp.zeros((1, N), F32)]
    for zz in range(nz):
        starts.append(starts[-1] + totals[zz])
    block_logs = list(totals)
    for b in range(zbits):
        rows = slice((ybits + b) * P_SIZE, (ybits + b + 1) * P_SIZE)
        for zz in range(nz):
            if (zz >> b) & 1:
                scale = jnp.exp2(starts[zz] - starts[(zz >> b) << b] + lead[zz])
                shi[slots[zz], rows, :] = (agg[(zz >> b) - 1] * scale).astype(BF16)
            else:
                shi[slots[zz], rows, :] = jnp.zeros((P_SIZE, N), BF16)
        pairs = range(len(agg) // 2)
        agg = [jnp.exp2(block_logs[2 * m + 1]) * agg[2 * m] + agg[2 * m + 1] for m in pairs]
        block_logs = [block_logs[2 * m] + block_logs[2 * m + 1] for m in pairs]


def shard_outputs(lev, r, skip, xb, bb, cb, gb, slow, tiles, shi, ob):
    hi = lev - 1 - LO
    half = Q // 2
    tri = lax.broadcasted_iota(jnp.int32, (half, half), 0) <= lax.broadcasted_iota(
        jnp.int32, (half, half), 1
    )

    def one(k, carry):
        at = span_at(k)
        x = xb[r, :, at].astype(F32)
        b = bb[r, at, :]
        c = cb[r, at, :]
        tile = tiles[r, k]
        cum = tile[0:1, :]
        cum_col = jnp.transpose(tile)[:, 0:1]
        xs = (x * tile[1:2, :]).astype(BF16)
        top = dot_nt(b[:half], c) * jnp.exp2(cum - cum_col[:half])
        low = dot_nt(b[half:], c[half:]) * jnp.exp2(cum[:, half:] - cum_col[half:])
        m00 = jnp.where(tri, top[:, :half], 0.0).astype(BF16)
        m01 = top[:, half:].astype(BF16)
        m11 = jnp.where(tri, low, 0.0).astype(BF16)
        left = dot(xs[:, :half], m00)
        right = dot(xs, jnp.concatenate([m01, m11], axis=0))
        local = jnp.concatenate([left, right], axis=1)
        lw = gb[r, :, at].astype(F32)
        r_lo = dot_nt(slow[r, k], c)
        r_hi = dot_nt(shi[r], c)
        e_lo = jnp.exp2(cum)
        e_hi = jnp.exp2(cum + tile[2:3, :])
        acc = local * lw[0:1] + skip * x
        for bit in range(LO):
            acc = acc + r_lo[bit * P_SIZE : (bit + 1) * P_SIZE] * (lw[1 + bit : 2 + bit] * e_lo)
        for bit in range(hi):
            row = 1 + LO + bit
            acc = acc + r_hi[bit * P_SIZE : (bit + 1) * P_SIZE] * (lw[row : row + 1] * e_hi)
        ob[r, :, at] = acc.astype(BF16)
        return carry

    lax.fori_loop(0, SPANS, one, 0, unroll=2)


def kernel(
    lev, sizes,
    x_ref, b_ref, c_ref, lg_ref, st_ref, lw_ref, skip_ref, out_ref,
    xb, bb, cb, gb, slow, tiles, sums, shi, ob, g_scr, st_scr, tmp, pk,
    l_own, l_x, l_o, s_x, r_x, s_g, r_g, s_z, r_z, s_n, r_n, s_f, r_f, s_s, r_s,
    s_m, r_m, s_o, r_o,
):
    nz, ny, nx, nc = sizes
    z, y, x, core = (lax.axis_index(a) for a in AXES)
    unit = SHARD // (nx * nc)
    rows = P_SIZE // ny
    other = 1 - core

    def turn(v, n):
        return lax.rem(v + n, n)

    def dev(dz=0, dy=0, dx=0, dc=0):
        return (turn(z + dz, nz), turn(y + dy, ny), turn(x + dx, nx), lax.rem(core + dc, nc))

    def rc(src, dst, send, recv, where):
        return pltpu.make_async_remote_copy(
            src_ref=src, dst_ref=dst, send_sem=send, recv_sem=recv,
            device_id=where, device_id_type=MESH,
        )

    def rel(i):
        odd = lax.rem(i, 2)
        return odd * ((i + 1) // 2) + (1 - odd) * lax.rem(nz - i // 2, nz)

    def cols(r, yy):
        at = (turn(z + r, nz) * ny + yy) * SHARD
        return pl.ds(pl.multiple_of(at, SHARD), SHARD)

    def band(yy):
        return pl.ds(pl.multiple_of(yy * rows, rows), rows)

    peers = [dev(dz=d) for d in range(1, nz)] + [dev(dy=d) for d in range(1, ny)]
    if nx > 1:
        peers += [dev(dx=1), dev(dx=-1)]
    if nc > 1:
        peers += [dev(dc=1)]
    barrier = pltpu.get_barrier_semaphore()
    for where in peers:
        pl.semaphore_signal(barrier, inc=1, device_id=where, device_id_type=MESH)

    src = (b_ref, c_ref)
    buf = (bb, cb)

    def piece(q, r, xx, cc, part=None):
        at = (xx * nc + cc) * unit
        size = unit
        if part is not None:
            size = unit // 2
            at = at + part * size
        return buf[q].at[r, pl.ds(pl.multiple_of(at, size), size), :]

    def own_copy(q):
        return pltpu.make_async_copy(src[q], piece(q, 0, x, core), l_own.at[q])

    def x_local(r):
        return pltpu.make_async_copy(x_ref.at[:, cols(r, y)], xb.at[r, band(y), :], l_x.at[r])

    def x_send(r, d):
        to = turn(y + d, ny)
        return rc(
            x_ref.at[:, cols(r, to)], xb.at[r, band(y), :],
            s_x.at[r, d - 1], r_x.at[r, d - 1], dev(dy=d),
        )

    def x_recv(r, d):
        to = turn(y + d, ny)
        return rc(
            x_ref.at[:, cols(r, to)], xb.at[r, band(turn(y - d, ny)), :],
            s_x.at[r, d - 1], r_x.at[r, d - 1], dev(dy=d),
        )

    def z_send(q, r):
        o = nz - r
        return rc(src[q], piece(q, r, x, core), s_z.at[q, r], r_z.at[q, r], dev(dz=o))

    def g_send(r):
        o = nz - r
        return rc(pk.at[turn(z + o, nz)], gb.at[r], s_g.at[r], r_g.at[r], dev(dz=o))

    def n_send(q, r, side, origin):
        part = piece(q, r, origin, core)
        return rc(part, part, s_n.at[q, side, r], r_n.at[q, side, r], dev(dx=1 - 2 * side))

    def f_send(q, r, side, origin):
        part = piece(q, r, origin, core, side)
        return rc(part, part, s_f.at[q, side, r], r_f.at[q, side, r], dev(dx=1 - 2 * side))

    def s_send(q, r, kind, cc):
        xx, part = ((0, None), (-1, None), (1, None), (-2, 0), (2, 1))[kind]
        ref = piece(q, r, turn(x + xx, nx), cc, part)
        return rc(ref, ref, s_s.at[q, kind, r], r_s.at[q, kind, r], dev(dc=1))

    kinds = 5 if nx > 1 else 1

    def step_a(q, i):
        r = rel(i)

        @pl.when(i == 0)
        def _():
            own_copy(q).wait()

        @pl.when(i > 0)
        def _():
            z_send(q, r).wait_recv()

        if nx > 1:
            n_send(q, r, 0, x).start()
            n_send(q, r, 1, x).start()
        if nc > 1:
            s_send(q, r, 0, core).start()

    def step_b(q, i):
        if nx > 1:
            r = rel(i)
            left, right = turn(x - 1, nx), turn(x + 1, nx)
            n_send(q, r, 0, left).wait_recv()
            f_send(q, r, 0, left).start()
            if nc > 1:
                s_send(q, r, 1, core).start()
            n_send(q, r, 1, right).wait_recv()
            f_send(q, r, 1, right).start()
            if nc > 1:
                s_send(q, r, 2, core).start()

    def step_c(q, i):
        if nx > 1:
            r = rel(i)
            far = turn(x + 2, nx)
            f_send(q, r, 0, far).wait_recv()
            if nc > 1:
                s_send(q, r, 3, core).start()
            f_send(q, r, 1, far).wait_recv()
            if nc > 1:
                s_send(q, r, 4, core).start()

    def step_s(q, i):
        if nc > 1:
            r = rel(i)
            for kind in range(kinds):
                s_send(q, r, kind, other).wait_recv()

    def m_send(r, d, yy):
        ref = sums.at[yy, r]
        return rc(ref, ref, s_m.at[r, d - 1], r_m.at[r, d - 1], dev(dy=d))

    def o_send(r, d):
        to = turn(y + d, ny)
        return rc(
            ob.at[r, band(to), :], out_ref.at[:, cols(r, y)],
            s_o.at[r, d - 1], r_o.at[r, d - 1], dev(dy=d),
        )

    def o_recv(r, d):
        to = turn(y + d, ny)
        return rc(
            ob.at[r, band(to), :], out_ref.at[:, cols(r, turn(y - d, ny))],
            s_o.at[r, d - 1], r_o.at[r, d - 1], dev(dy=d),
        )

    def o_local(r):
        return pltpu.make_async_copy(ob.at[r, band(y), :], out_ref.at[:, cols(r, y)], l_o.at[r])

    own_copy(0).start()
    own_copy(1).start()
    pack_gates(lev, z, lw_ref, lg_ref, st_ref, tmp, pk)
    gb[0] = pk[z]
    pl.semaphore_wait(barrier, len(peers))

    def begin(i, carry):
        r = rel(i)

        @pl.when(i > 0)
        def _():
            z_send(0, r).start()
            pack_gates(lev, turn(z - r, nz), lw_ref, lg_ref, st_ref, tmp, pk)
            g_send(r).start()

        x_local(r).start()
        for d in range(1, ny):
            x_send(r, d).start()
        return carry

    lax.fori_loop(0, nz, begin, 0)

    def inward(i, carry):
        @pl.when(i < nz)
        def _():
            step_a(0, i)

        @pl.when((i >= 1) & (i <= nz))
        def _():
            step_b(0, i - 1)

        @pl.when((i >= 2) & (i <= nz + 1))
        def _():
            step_c(0, i - 2)

        @pl.when((i >= 3) & (i <= nz + 1))
        def _():
            z_send(1, rel(i - 2)).start()

        @pl.when((i >= nz) & (i < 2 * nz))
        def _():
            step_a(1, i - nz)

        @pl.when(i >= nz + 1)
        def _():
            step_b(1, i - nz - 1)

        @pl.when(i >= nz + 2)
        def _():
            step_c(1, i - nz - 2)

        @pl.when(i >= 3)
        def _():
            r = rel(i - 3)
            step_s(0, i - 3)

            @pl.when(i > 3)
            def _():
                g_send(r).wait_recv()

            x_local(r).wait()
            for d in range(1, ny):
                x_recv(r, d).wait_recv()
            state, log = shard_states(lev, r, xb, bb, gb, slow, tiles, g_scr, st_scr)
            sums[y, r, 0:P_SIZE, :] = state
            sums[y, r, P_SIZE : P_SIZE + 8, :] = jnp.broadcast_to(log, (8, N))
            for d in range(1, ny):
                m_send(r, d, y).start()

        return carry

    lax.fori_loop(0, nz + 3, inward, 0)

    def gather(r, carry):
        for d in range(1, ny):
            m_send(r, d, turn(y - d, ny)).wait_recv()
        return carry

    lax.fori_loop(0, nz, gather, 0)
    shard_levels(nz, ny, z, y, sums, shi)
    skip = skip_ref[z]
    early = min(3, nz)

    def outward(i, carry):
        r = rel(i)

        @pl.when(i + early < nz)
        def _():
            step_a(1, i + early)

        @pl.when(i + 2 < nz)
        def _():
            step_b(1, i + 2)

        @pl.when(i + 1 < nz)
        def _():
            step_c(1, i + 1)

        step_s(1, i)
        shard_outputs(lev, r, skip, xb, bb, cb, gb, slow, tiles, shi, ob)
        o_local(r).start()
        for d in range(1, ny):
            o_send(r, d).start()
        return carry

    lax.fori_loop(0, nz, outward, 0)

    def finish(r, carry):
        @pl.when(r > 0)
        def _():
            g_send(r).wait_send()
            for q in range(2):
                z_send(q, r).wait_send()

        for q in range(2):
            if nx > 1:
                for side in range(2):
                    n_send(q, r, side, x).wait_send()
                    f_send(q, r, side, x).wait_send()
            if nc > 1:
                for kind in range(kinds):
                    s_send(q, r, kind, core).wait_send()
        for d in range(1, ny):
            x_send(r, d).wait_send()
            m_send(r, d, y).wait_send()
            o_send(r, d).wait_send()
        for d in range(1, ny):
            o_recv(r, d).wait_recv()
        o_local(r).wait()
        return carry

    lax.fori_loop(0, nz, finish, 0)


def on_device(x_heads, b_proj, c_proj, log_gate, step_size, level_weight, skip):
    nz, ny, nx, nc = sizes = tuple(lax.axis_size(a) for a in AXES)
    lev = level_weight.shape[1]
    hi = lev - 1 - LO
    rows, tok = x_heads.shape
    any_spec = pl.BlockSpec(memory_space=pl.ANY)
    vmem = pl.BlockSpec(memory_space=pltpu.VMEM)
    dma = lambda *shape: pltpu.SemaphoreType.DMA(shape)
    ys = max(ny - 1, 1)
    return pl.pallas_call(
        functools.partial(kernel, lev, sizes),
        out_shape=jax.ShapeDtypeStruct((rows, tok), BF16),
        in_specs=[any_spec, any_spec, any_spec, vmem, vmem, vmem,
                  pl.BlockSpec(memory_space=pltpu.SMEM)],
        out_specs=any_spec,
        scratch_shapes=[
            pltpu.VMEM((nz, P_SIZE, SHARD), BF16),
            pltpu.VMEM((nz, SHARD, N), BF16),
            pltpu.VMEM((nz, SHARD, N), BF16),
            pltpu.VMEM((nz, 16, SHARD), BF16),
            pltpu.VMEM((nz, SPANS, LO * P_SIZE, N), BF16),
            pltpu.VMEM((nz, SPANS, 8, Q), F32),
            pltpu.VMEM((ny, nz, P_SIZE + 8, N), F32),
            pltpu.VMEM((nz, hi * P_SIZE, N), BF16),
            pltpu.VMEM((nz, P_SIZE, SHARD), BF16),
            pltpu.VMEM((4, SPANS, Q), F32),
            pltpu.VMEM((SPANS, P_SIZE, N), F32),
            pltpu.VMEM((16, SHARD), F32),
            pltpu.VMEM((nz, 16, SHARD), BF16),
            dma(2), dma(nz), dma(nz),
            dma(nz, ys), dma(nz, ys),
            dma(nz), dma(nz),
            dma(2, nz), dma(2, nz),
            dma(2, 2, nz), dma(2, 2, nz),
            dma(2, 2, nz), dma(2, 2, nz),
            dma(2, 5, nz), dma(2, 5, nz),
            dma(nz, ys), dma(nz, ys),
            dma(nz, ys), dma(nz, ys),
        ],
        compiler_params=pltpu.CompilerParams(
            collective_id=0, has_side_effects=True, vmem_limit_bytes=56 << 20
        ),
        name="layer",
    )(x_heads, b_proj, c_proj, log_gate, step_size, level_weight, skip)


def build(mesh):
    group = ("x", "core")
    seq = ("z", "y")
    in_specs = (
        P(group + seq, None),
        P(seq + group, None),
        P(seq + group, None),
        P(group, seq),
        P(group, seq),
        P(group, None, seq),
        P(group),
    )
    return jax.shard_map(
        on_device, mesh=mesh, in_specs=in_specs, out_specs=P(group + seq, None), check_vma=False
    )


def solution(mesh):
    return build(Mesh(mesh.devices.reshape(8, 4, 4, 2), AXES))
```

time: 393 us -> 148 us (0.38)
  waiting for transfers between devices: 162 us -> 0 us
  blocking collectives: 62.3 us -> 0 us
  Pallas kernels: 91 us -> 139 us
  local copies, waits for them, and re-layouts: 45.3 us -> 7.91 us
  starting transfers between devices: 13.7 us -> 0 us
  between operations: 13.3 us -> 0.01 us
    all_gather x3 -> x0, waiting for transfers between devices: 94.7 us -> none  [the longest x1 82.6 us: on_device(): c = lax.all_gather(c_proj, ('z', 'x', 'core'), axis=0, tiled=True)]
    all_to_all x2 -> x0, waiting for transfers between devices: 66.1 us -> none  [the longest x1 41.5 us: on_device(): lax.all_to_all(x, 'y', split_axis=2, concat_axis=0, tiled=True)]
    all_to_all x1 -> x0, blocking collectives: 53.3 us -> none  [on_device(): out = lax.all_to_all(out, 'y', split_axis=0, concat_axis=2, tiled=True)]
    pallas_call x2 -> x1, Pallas kernels: 91 us -> 139 us  [on_device(): pl.pallas_call(functools.partial(kernel, lev, sizes), out_shape=jax.Shape...]
    reshape x4 -> x0, local copies, waits for them, and re-layouts: 19.3 us -> none  [the longest x2 13.2 us: on_device(): x = x_heads.reshape(rows, nz, ny, SHARD)]
    all_to_all x2 -> x0, starting transfers between devices: 13.6 us -> none  [the longest x1 8.57 us: on_device(): gates = lax.all_to_all(packed, 'z', split_axis=0, concat_axis=0, tiled=True)]
    all_gather x1 -> x0, blocking collectives: 8.99 us -> none  [on_device(): logs = lax.all_gather(total[:, 0, 0], 'y', axis=1).reshape(nz * ny)]
    another operation x9 -> x0, local copies, waits for them, and re-layouts: 7.52 us -> none  [the longest x7 7.07 us: on_device(): packed = jnp.stack(parts, axis=1).astype(BF16)]
  transfers between devices with their start and end apart: 5 -> 0, of which waited for: 4 -> 0; matrix products, arithmetic and copies ran while one was open for 8% -> 0% of each run, Pallas kernels for 0% -> 0%
where the time goes in v2:
time: 148 us; the launch traced here: 147 us
  Pallas kernels  139 us (94%)
  local copies, waits for them, and re-layouts  7.91 us (5%)
    pallas_call x1, Pallas kernels, on_device(): pl.pallas_call(functools.partial(kernel, lev, sizes), out_shape=jax.Shape...  139 us
    unnamed x2, local copies, waits for them, and re-layouts  7.91 us

profile of v2, /device:TPU:32, one launch (start us, length us, event | category | flops | bytes accessed | tf_op | source)
XLA Modules:
  0.0 147.4 jit_solution(410646184816967227)
XLA Ops:
  0.0 3.4 %copy.8.lw_ref = f32[8,10,4096]{2,1,0:T(8,128)} copy(f32[8,10,4096]{2,0,1:T(8,128)} %param.12) | data formatting | bytes 2621440 | tf_op args[5]
  3.4 139.4 %layer.1 = bf16[16,131072]{1,0:T(8,128)(2,1)} custom-call(bf16[16,131072]{1,0:T(8,128)(2,1)} %x_ref.1, bf16[512,128]{1,0:T(8,128)(2,1)} %b_ref.1, bf16[512,128]{1,0:T(8,128)(2,1)} %c_ref.1, f32[8,4096]{1,0:T(8,128)} %lg_ref.1, f32[8,4096]{1,0:T(8,128)} %st_ref.1, f32[8,10,4096]{2,1,0:T(8,128)} %copy.8.lw_ref, f32[8]{0:T(128)} %skip_ref.1), custom_call_target="tpu_custom_call" | custom-call | tf_op jit(solution)/shard_map/layer/pallas_call | solution.py:501
  142.9 4.5 %copy.10 = bf16[16,131072]{1,0:T(8,128)(2,1)} copy(bf16[16,131072]{1,0:T(8,128)(2,1)} %layer.1) | data formatting | bytes 8388608

commit v3 on v2

v3 whole, which is shorter than its diff:
```python
import functools

import jax
import jax.numpy as jnp
from jax import lax
from jax.experimental import pallas as pl
from jax.experimental.pallas import tpu as pltpu
from jax.sharding import Mesh, PartitionSpec as P

P_SIZE = 64
N = 128
Q = 256
LO = 4
SPANS = 1 << LO
SHARD = SPANS * Q
LOG2E = 1.4426950408889634
NT = (((1,), (1,)), ((), ()))
F32 = jnp.float32
BF16 = jnp.bfloat16
MESH = pl.DeviceIdType.MESH
AXES = ("z", "y", "x", "core")


def dot(a, b):
    return jnp.dot(a, b, preferred_element_type=F32)


def dot_nt(a, b):
    return lax.dot_general(a, b, NT, preferred_element_type=F32)


def span_at(k):
    return pl.ds(pl.multiple_of(k * Q, Q), Q)


def pack_gates(lev, h, lw_ref, lg_ref, st_ref, tmp, pk):
    for row in range(lev):
        tmp[row : row + 1, :] = lw_ref[row, pl.ds(h, 1), :]
    for row, ref in ((lev, lg_ref), (lev + 3, st_ref)):
        v = ref[pl.ds(h, 1), :]
        first = v.astype(BF16).astype(F32)
        rest = v - first
        second = rest.astype(BF16).astype(F32)
        tmp[row : row + 1, :] = first
        tmp[row + 1 : row + 2, :] = second
        tmp[row + 2 : row + 3, :] = rest - second
    pk[h] = tmp[...].astype(BF16)


def shard_states(lev, r, xb, bb, gb, slow, tiles, g_scr, st_scr):
    for k in range(SPANS):
        piece = gb[r, :, k * Q : (k + 1) * Q].astype(F32)
        for m in range(3):
            g_scr[m, k : k + 1, :] = piece[lev + m : lev + m + 1]
        g_scr[3, k : k + 1, :] = (
            piece[lev + 3 : lev + 4] + piece[lev + 4 : lev + 5] + piece[lev + 5 : lev + 6]
        )
    upper = (
        lax.broadcasted_iota(jnp.int32, (Q, Q), 0) <= lax.broadcasted_iota(jnp.int32, (Q, Q), 1)
    ).astype(BF16)
    cum = dot(g_scr[0].astype(BF16), upper)
    cum = cum + dot(g_scr[1].astype(BF16), upper)
    cum = (cum + dot(g_scr[2].astype(BF16), upper)) * LOG2E
    step = g_scr[3]
    g_scr[0] = jnp.exp2(cum[:, Q - 1 :] - cum) * step
    logs = [jnp.broadcast_to(cum[k : k + 1, Q - 1 :], (1, N)) for k in range(SPANS)]
    starts = [jnp.zeros((1, N), F32)]
    for k in range(SPANS):
        starts.append(starts[-1] + logs[k])
    for k in range(SPANS):
        tiles[r, k, 0:1, :] = cum[k : k + 1]
        tiles[r, k, 1:2, :] = step[k : k + 1]
        tiles[r, k, 2:3, :] = jnp.concatenate([starts[k], starts[k]], axis=1)

    def one(k, carry):
        w = xb[r, :, span_at(k)].astype(F32) * g_scr[0, pl.ds(k, 1), :]
        st_scr[k] = dot(w.astype(BF16), bb[r, span_at(k), :])
        return carry

    lax.fori_loop(0, SPANS, one, 0, unroll=2)
    agg = [st_scr[k] for k in range(SPANS)]
    block_logs = list(logs)
    for bit in range(LO):
        rows = slice(bit * P_SIZE, (bit + 1) * P_SIZE)
        for k in range(SPANS):
            if (k >> bit) & 1:
                scale = jnp.exp2(starts[k] - starts[(k >> bit) << bit])
                slow[r, k, rows, :] = (agg[(k >> bit) - 1] * scale).astype(BF16)
            else:
                slow[r, k, rows, :] = jnp.zeros((P_SIZE, N), BF16)
        pairs = range(len(agg) // 2)
        agg = [jnp.exp2(block_logs[2 * m + 1]) * agg[2 * m] + agg[2 * m + 1] for m in pairs]
        block_logs = [block_logs[2 * m] + block_logs[2 * m + 1] for m in pairs]
    return agg[0], block_logs[0]


def shard_levels(nz, ny, z, y, sums, shi):
    ybits = ny.bit_length() - 1
    zbits = nz.bit_length() - 1
    slots = [lax.rem(zz - z + nz, nz) for zz in range(nz)]
    before = [jnp.where(yy < y, 1.0, 0.0) for yy in range(ny)]
    belongs = []
    for b in range(ybits):
        own = y // (1 << b)
        odd = lax.rem(own, 2) == 1
        belongs.append(
            [jnp.where(odd & (own - 1 == yy >> b), 1.0, 0.0) for yy in range(ny)]
        )
    agg, totals, lead = [], [], []
    for zz in range(nz):
        logs = []
        for yy in range(ny):
            block = sums[yy, slots[zz], P_SIZE : P_SIZE + 16, :].astype(F32)
            logs.append(block[0:1] + block[1:2] + block[2:3])
        ahead = logs[0] * before[0]
        for yy in range(1, ny):
            ahead = ahead + logs[yy] * before[yy]
        lead.append(ahead)
        after = jnp.zeros((1, N), F32)
        near = jnp.zeros((1, N), F32)
        whole = None
        parts = [None] * ybits
        for yy in reversed(range(ny)):
            state = sums[yy, slots[zz], 0:P_SIZE, :].astype(F32)
            term = state * jnp.exp2(after)
            whole = term if whole is None else whole + term
            scale = jnp.exp2(near)
            for b in range(ybits):
                term = state * (scale * belongs[b][yy])
                parts[b] = term if parts[b] is None else parts[b] + term
            after = after + logs[yy]
            near = near + logs[yy] * before[yy]
        agg.append(whole)
        totals.append(after)
        for b in range(ybits):
            shi[slots[zz], b * P_SIZE : (b + 1) * P_SIZE, :] = parts[b].astype(BF16)
    starts = [jnp.zeros((1, N), F32)]
    for zz in range(nz):
        starts.append(starts[-1] + totals[zz])
    block_logs = list(totals)
    for b in range(zbits):
        rows = slice((ybits + b) * P_SIZE, (ybits + b + 1) * P_SIZE)
        for zz in range(nz):
            if (zz >> b) & 1:
                scale = jnp.exp2(starts[zz] - starts[(zz >> b) << b] + lead[zz])
                shi[slots[zz], rows, :] = (agg[(zz >> b) - 1] * scale).astype(BF16)
            else:
                shi[slots[zz], rows, :] = jnp.zeros((P_SIZE, N), BF16)
        pairs = range(len(agg) // 2)
        agg = [jnp.exp2(block_logs[2 * m + 1]) * agg[2 * m] + agg[2 * m + 1] for m in pairs]
        block_logs = [block_logs[2 * m] + block_logs[2 * m + 1] for m in pairs]


def span_mix(k, r, bb, cb, tiles, mix, slot):
    half = Q // 2
    tri = lax.broadcasted_iota(jnp.int32, (half, half), 0) <= lax.broadcasted_iota(
        jnp.int32, (half, half), 1
    )
    at = span_at(k)
    b = bb[r, at, :]
    c = cb[r, at, :]
    tile = tiles[r, k]
    cum = tile[0:1, :]
    cum_col = jnp.transpose(tile)[:, 0:1]
    top = dot_nt(b[:half], c) * jnp.exp2(cum - cum_col[:half])
    low = dot_nt(b[half:], c[half:]) * jnp.exp2(cum[:, half:] - cum_col[half:])
    mix[slot, :half, :half] = jnp.where(tri, top[:, :half], 0.0).astype(BF16)
    mix[slot, :half, half:] = top[:, half:].astype(BF16)
    mix[slot, half:, half:] = jnp.where(tri, low, 0.0).astype(BF16)


def span_out(lev, k, r, skip, xb, cb, gb, slow, tiles, shi, ob, mix, slot):
    hi = lev - 1 - LO
    at = span_at(k)
    x = xb[r, :, at].astype(F32)
    c = cb[r, at, :]
    tile = tiles[r, k]
    cum = tile[0:1, :]
    xs = (x * tile[1:2, :]).astype(BF16)
    lw = gb[r, :, at].astype(F32)
    acc = dot(xs, mix[slot]) * lw[0:1] + skip * x
    r_lo = dot_nt(slow[r, k], c)
    r_hi = dot_nt(shi[r], c)
    e_lo = jnp.exp2(cum)
    e_hi = jnp.exp2(cum + tile[2:3, :])
    for bit in range(LO):
        acc = acc + r_lo[bit * P_SIZE : (bit + 1) * P_SIZE] * (lw[1 + bit : 2 + bit] * e_lo)
    for bit in range(hi):
        row = 1 + LO + bit
        acc = acc + r_hi[bit * P_SIZE : (bit + 1) * P_SIZE] * (lw[row : row + 1] * e_hi)
    ob[r, :, at] = acc.astype(BF16)


def shard_outputs(lev, r, first, count, skip, xb, bb, cb, gb, slow, tiles, shi, ob, mix):
    span_mix(first, r, bb, cb, tiles, mix, 0)

    def two(m, carry):
        k = first + 2 * m
        span_out(lev, k, r, skip, xb, cb, gb, slow, tiles, shi, ob, mix, 0)
        span_mix(k + 1, r, bb, cb, tiles, mix, 1)
        span_out(lev, k + 1, r, skip, xb, cb, gb, slow, tiles, shi, ob, mix, 1)
        span_mix(jnp.minimum(k + 2, first + count - 1), r, bb, cb, tiles, mix, 0)
        return carry

    lax.fori_loop(0, count // 2, two, 0)


def kernel(
    lev, sizes,
    x_ref, b_ref, c_ref, lg_ref, st_ref, lw_ref, skip_ref, out_ref,
    xb, bb, cb, gb, slow, tiles, sums, shi, ob, g_scr, st_scr, tmp, pk, mix, lwb, rowb,
    l_own, l_o, sent, r_x, r_g, r_z, r_h, r_n, r_f, r_s, r_m, r_o,
):
    nz, ny, nx, nc = sizes
    z, y, x, core = (lax.axis_index(a) for a in AXES)
    unit = SHARD // (nx * nc)
    rows = P_SIZE // ny
    other = 1 - core

    def turn(v, n):
        return lax.rem(v + n, n)

    def dev(dz=0, dy=0, dx=0, dc=0):
        return (turn(z + dz, nz), turn(y + dy, ny), turn(x + dx, nx), lax.rem(core + dc, nc))

    def rc(src, dst, send, recv, where):
        return pltpu.make_async_remote_copy(
            src_ref=src, dst_ref=dst, send_sem=send, recv_sem=recv,
            device_id=where, device_id_type=MESH,
        )

    def rel(i):
        odd = lax.rem(i, 2)
        return odd * ((i + 1) // 2) + (1 - odd) * lax.rem(nz - i // 2, nz)

    def cols(r, yy):
        at = (turn(z + r, nz) * ny + yy) * SHARD
        return pl.ds(pl.multiple_of(at, SHARD), SHARD)

    def band(yy):
        return pl.ds(pl.multiple_of(yy * rows, rows), rows)

    peers = [dev(dz=d) for d in range(1, nz)] + [dev(dy=d) for d in range(1, ny)]
    if nx > 1:
        peers += [dev(dx=1), dev(dx=-1)]
    if nc > 1:
        peers += [dev(dc=1)]
    barrier = pltpu.get_barrier_semaphore()
    for where in peers:
        pl.semaphore_signal(barrier, inc=1, device_id=where, device_id_type=MESH)

    src = (b_ref, c_ref)
    buf = (bb, cb)

    def piece(q, r, xx, cc, part=None):
        at = (xx * nc + cc) * unit
        size = unit
        if part is not None:
            size = unit // 2
            at = at + part * size
        return buf[q].at[r, pl.ds(pl.multiple_of(at, size), size), :]

    def own_copy(q):
        return pltpu.make_async_copy(src[q], piece(q, 0, x, core), l_own.at[q])

    def x_local(r):
        return pltpu.make_async_copy(x_ref.at[:, cols(r, y)], xb.at[r, band(y), :], r_x.at[r])

    def x_send(r, d):
        to = turn(y + d, ny)
        return rc(
            x_ref.at[:, cols(r, to)], xb.at[r, band(y), :], sent.at[0], r_x.at[r], dev(dy=d)
        )

    def bulk(ref, send, recv):
        return rc(ref, ref, send, recv, peers[0])

    def some(q, count):
        if count % SHARD == 0:
            return buf[q].at[pl.ds(0, count // SHARD)]
        return buf[q].at[0, pl.ds(0, count), :]

    mid = nz // 2

    def z_send(q, r, side, part=None):
        to = lax.rem(r - 1 + nz, nz) if side == 0 else r + 1
        arrived = r_z.at[q, to] if part is None or side == 0 else r_h.at[q]
        return rc(
            piece(q, r, x, core, part), piece(q, to, x, core, part),
            sent.at[4 + q], arrived, dev(dz=1 - 2 * side),
        )

    def z_each(q, r, act):
        ahead = lax.rem(nz - r, nz)

        @pl.when(((r == 0) | (r > mid)) & (ahead + 1 < mid))
        def _():
            act(z_send(q, r, 0))

        @pl.when(((r == 0) | (r > mid)) & (ahead + 1 == mid))
        def _():
            act(z_send(q, r, 0, 0))

        @pl.when(r + 1 < mid)
        def _():
            act(z_send(q, r, 1))

        @pl.when(r + 1 == mid)
        def _():
            act(z_send(q, r, 1, 1))

    def z_wait(q, r):
        @pl.when(r != mid)
        def _():
            ref = piece(q, r, x, core)
            rc(ref, ref, sent.at[4 + q], r_z.at[q, r], dev(dz=1)).wait_recv()

        @pl.when(r == mid)
        def _():
            ref = piece(q, r, x, core, 0)
            rc(ref, ref, sent.at[4 + q], r_z.at[q, r], dev(dz=1)).wait_recv()
            ref = piece(q, r, x, core, 1)
            rc(ref, ref, sent.at[4 + q], r_h.at[q], dev(dz=-1)).wait_recv()

    def g_send(r):
        o = nz - r
        return rc(pk.at[turn(z + o, nz)], gb.at[r], sent.at[1], r_g.at[r], dev(dz=o))

    def n_send(q, r, side, origin):
        part = piece(q, r, origin, core)
        return rc(part, part, sent.at[6 + q], r_n.at[q, r], dev(dx=1 - 2 * side))

    def f_send(q, r, side, origin):
        part = piece(q, r, origin, core, side)
        return rc(part, part, sent.at[8 + q], r_f.at[q, r], dev(dx=1 - 2 * side))

    def s_send(q, r, kind, cc):
        xx, part = ((0, None), (-1, None), (1, None), (-2, 0), (2, 1))[kind]
        ref = piece(q, r, turn(x + xx, nx), cc, part)
        return rc(ref, ref, sent.at[10 + q], r_s.at[q, r], dev(dc=1))

    kinds = 5 if nx > 1 else 1

    def step_a(q, i):
        r = rel(i)

        @pl.when(i == 0)
        def _():
            own_copy(q).wait()

        @pl.when(i > 0)
        def _():
            z_wait(q, r)

        z_each(q, r, lambda copy: copy.start())

        if nx > 1:
            n_send(q, r, 0, x).start()
            n_send(q, r, 1, x).start()
        if nc > 1:
            s_send(q, r, 0, core).start()

    def step_b(q, i):
        if nx > 1:
            r = rel(i)
            bulk(some(q, 2 * unit), sent.at[6 + q], r_n.at[q, r]).wait_recv()
            for side, origin in ((0, turn(x - 1, nx)), (1, turn(x + 1, nx))):
                f_send(q, r, side, origin).start()
                if nc > 1:
                    s_send(q, r, 1 + side, core).start()

    def step_c(q, i):
        if nx > 1:
            r = rel(i)
            bulk(some(q, unit), sent.at[8 + q], r_f.at[q, r]).wait_recv()
            if nc > 1:
                for kind in (3, 4):
                    s_send(q, r, kind, core).start()

    def step_s(q, i):
        if nc > 1:
            r = rel(i)
            bulk(some(q, nx * unit), sent.at[10 + q], r_s.at[q, r]).wait_recv()

    def m_send(r, d):
        ref = sums.at[y, r]
        return rc(ref, ref, sent.at[2], r_m.at[0], dev(dy=d))

    part_size = SHARD // 2

    def out_cols(r, part, yy):
        at = (turn(z + r, nz) * ny + yy) * SHARD + part * part_size
        return pl.ds(pl.multiple_of(at, part_size), part_size)

    def here(part):
        return pl.ds(pl.multiple_of(part * part_size, part_size), part_size)

    def o_send(r, part, d):
        to = turn(y + d, ny)
        return rc(
            ob.at[r, band(to), here(part)], out_ref.at[:, out_cols(r, part, y)],
            sent.at[3], r_o.at[0], dev(dy=d),
        )

    def o_local(r, part):
        return pltpu.make_async_copy(
            ob.at[r, band(y), here(part)], out_ref.at[:, out_cols(r, part, y)], l_o.at[0]
        )

    loads = [
        pltpu.make_async_copy(lw_ref, lwb, l_own.at[2]),
        pltpu.make_async_copy(lg_ref, rowb.at[0], l_own.at[3]),
        pltpu.make_async_copy(st_ref, rowb.at[1], l_own.at[4]),
    ]
    own_copy(0).start()
    own_copy(1).start()
    for copy in loads:
        copy.start()
    mix[...] = jnp.zeros_like(mix)
    pl.semaphore_wait(barrier, len(peers))

    def begin(i, carry):
        r = rel(i)
        x_local(r).start()
        for d in range(1, ny):
            x_send(r, d).start()
        return carry

    lax.fori_loop(0, nz, begin, 0)
    step_a(0, 0)
    for copy in loads:
        copy.wait()
    pack_gates(lev, z, lwb, rowb.at[0], rowb.at[1], tmp, pk)
    gb[0] = pk[z]

    def inward(i, carry):
        @pl.when((i >= 1) & (i < nz))
        def _():
            step_a(0, i)

        @pl.when((i >= 1) & (i <= nz))
        def _():
            step_b(0, i - 1)

        @pl.when((i >= 2) & (i <= nz + 1))
        def _():
            step_c(0, i - 2)

        @pl.when((i >= 1) & (i < nz))
        def _():
            r = rel(i)
            pack_gates(lev, turn(z - r, nz), lwb, rowb.at[0], rowb.at[1], tmp, pk)
            g_send(r).start()

        @pl.when((i >= nz) & (i < 2 * nz))
        def _():
            step_a(1, i - nz)

        @pl.when(i >= nz + 1)
        def _():
            step_b(1, i - nz - 1)

        @pl.when(i >= nz + 2)
        def _():
            step_c(1, i - nz - 2)

        @pl.when(i >= 3)
        def _():
            r = rel(i - 3)
            step_s(0, i - 3)

            @pl.when(i > 3)
            def _():
                g_send(r).wait_recv()

            bulk(xb.at[r], sent.at[0], r_x.at[r]).wait_recv()
            state, log = shard_states(lev, r, xb, bb, gb, slow, tiles, g_scr, st_scr)
            sums[y, r, 0:P_SIZE, :] = state.astype(BF16)
            first = log.astype(BF16).astype(F32)
            rest = log - first
            second = rest.astype(BF16).astype(F32)
            logs = jnp.concatenate([first, second, rest - second, jnp.zeros((13, N), F32)], axis=0)
            sums[y, r, P_SIZE : P_SIZE + 16, :] = logs.astype(BF16)
            for d in range(1, ny):
                m_send(r, d).start()

        return carry

    lax.fori_loop(1, nz + 3, inward, 0)

    bulk(sums.at[pl.ds(0, ny - 1)], sent.at[2], r_m.at[0]).wait_recv()
    shard_levels(nz, ny, z, y, sums, shi)
    skip = skip_ref[z]
    early = min(3, nz)

    def outward(j, carry):
        i, part = j // 2, lax.rem(j, 2)
        r = rel(i)

        @pl.when(part == 0)
        def _():
            @pl.when(i + early < nz)
            def _():
                step_a(1, i + early)

            @pl.when(i + 2 < nz)
            def _():
                step_b(1, i + 2)

            @pl.when(i + 1 < nz)
            def _():
                step_c(1, i + 1)

            step_s(1, i)

        half = SPANS // 2
        shard_outputs(
            lev, r, part * half, half, skip, xb, bb, cb, gb, slow, tiles, shi, ob, mix
        )
        o_local(r, part).start()
        for d in range(1, ny):
            o_send(r, part, d).start()
        return carry

    lax.fori_loop(0, 2 * nz, outward, 0)

    away = nz * (ny - 1) * rows * SHARD // (P_SIZE * SHARD)
    bulk(xb.at[pl.ds(0, away)], sent.at[0], r_x.at[0]).wait_send()
    bulk(pk.at[pl.ds(0, nz - 1)], sent.at[1], r_g.at[0]).wait_send()
    bulk(sums.at[pl.ds(0, ny - 1)], sent.at[2], r_m.at[0]).wait_send()
    bulk(ob.at[pl.ds(0, away)], sent.at[3], r_o.at[0]).wait_send()
    for q in range(2):
        bulk(some(q, (nz - 1) * unit), sent.at[4 + q], r_h.at[q]).wait_send()
        if nx > 1:
            bulk(some(q, 2 * nz * unit), sent.at[6 + q], r_h.at[q]).wait_send()
            bulk(some(q, nz * unit), sent.at[8 + q], r_h.at[q]).wait_send()
        if nc > 1:
            bulk(some(q, nx * nz * unit), sent.at[10 + q], r_h.at[q]).wait_send()
    bulk(ob.at[pl.ds(0, away)], sent.at[3], r_o.at[0]).wait_recv()
    mine = ob.at[pl.ds(0, nz // ny)]
    pltpu.make_async_copy(mine, mine, l_o.at[0]).wait()


def on_device(x_heads, b_proj, c_proj, log_gate, step_size, level_weight, skip):
    nz, ny, nx, nc = sizes = tuple(lax.axis_size(a) for a in AXES)
    lev = level_weight.shape[1]
    hi = lev - 1 - LO
    rows, tok = x_heads.shape
    any_spec = pl.BlockSpec(memory_space=pl.ANY)
    dma = lambda *shape: pltpu.SemaphoreType.DMA(shape)
    return pl.pallas_call(
        functools.partial(kernel, lev, sizes),
        out_shape=jax.ShapeDtypeStruct((rows, tok), BF16),
        in_specs=[any_spec, any_spec, any_spec, any_spec, any_spec, any_spec,
                  pl.BlockSpec(memory_space=pltpu.SMEM)],
        out_specs=any_spec,
        scratch_shapes=[
            pltpu.VMEM((nz, P_SIZE, SHARD), BF16),
            pltpu.VMEM((nz, SHARD, N), BF16),
            pltpu.VMEM((nz, SHARD, N), BF16),
            pltpu.VMEM((nz, 16, SHARD), BF16),
            pltpu.VMEM((nz, SPANS, LO * P_SIZE, N), BF16),
            pltpu.VMEM((nz, SPANS, 8, Q), F32),
            pltpu.VMEM((ny, nz, P_SIZE + 16, N), BF16),
            pltpu.VMEM((nz, hi * P_SIZE, N), BF16),
            pltpu.VMEM((nz, P_SIZE, SHARD), BF16),
            pltpu.VMEM((4, SPANS, Q), F32),
            pltpu.VMEM((SPANS, P_SIZE, N), F32),
            pltpu.VMEM((16, SHARD), F32),
            pltpu.VMEM((nz, 16, SHARD), BF16),
            pltpu.VMEM((2, Q, Q), BF16),
            pltpu.VMEM((lev, nz, SHARD), F32),
            pltpu.VMEM((2, nz, SHARD), F32),
            dma(5), dma(1), dma(12),
            dma(nz), dma(nz), dma(2, nz), dma(2), dma(2, nz), dma(2, nz), dma(2, nz), dma(1), dma(1),
        ],
        compiler_params=pltpu.CompilerParams(
            collective_id=0, has_side_effects=True, vmem_limit_bytes=56 << 20
        ),
        name="layer",
    )(x_heads, b_proj, c_proj, log_gate, step_size, jnp.swapaxes(level_weight, 0, 1), skip)


def build(mesh):
    group = ("x", "core")
    seq = ("z", "y")
    in_specs = (
        P(group + seq, None),
        P(seq + group, None),
        P(seq + group, None),
        P(group, seq),
        P(group, seq),
        P(group, None, seq),
        P(group),
    )
    return jax.shard_map(
        on_device, mesh=mesh, in_specs=in_specs, out_specs=P(group + seq, None), check_vma=False
    )


def solution(mesh):
    return build(Mesh(mesh.devices.reshape(8, 4, 4, 2), AXES))
```

time: 148 us -> 123 us (0.83); the launches traced: 147 us -> 120 us
  Pallas kernels: 139 us -> 116 us
  local copies, waits for them, and re-layouts: 7.91 us -> 4.47 us
    pallas_call x1, Pallas kernels: 139 us -> 116 us  [on_device(): pl.pallas_call(functools.partial(kernel, lev, sizes), out_shape=jax.Shape...]
    unnamed x2 -> x1, local copies, waits for them, and re-layouts: 7.91 us -> 4.47 us
where the time goes in v3:
time: 123 us; the launch traced here: 120 us
  Pallas kernels  116 us (94%)
  local copies, waits for them, and re-layouts  4.47 us (4%)
    pallas_call x1, Pallas kernels, on_device(): pl.pallas_call(functools.partial(kernel, lev, sizes), out_shape=jax.Shape...  116 us
    unnamed x1, local copies, waits for them, and re-layouts  4.47 us

profile of v3, /device:TPU:32, one launch (start us, length us, event | category | flops | bytes accessed | tf_op | source)
XLA Modules:
  0.0 120.4 jit_solution(16013581999524511923)
XLA Ops:
  0.0 115.9 %layer.1 = bf16[16,131072]{1,0:T(8,128)(2,1)} custom-call(bf16[16,131072]{1,0:T(8,128)(2,1)} %x_ref.1, bf16[512,128]{1,0:T(8,128)(2,1)} %b_ref.1, bf16[512,128]{1,0:T(8,128)(2,1)} %c_ref.1, f32[8,4096]{1,0:T(8,128)} %lg_ref.1, f32[8,4096]{1,0:T(8,128)} %st_ref.1, f32[10,8,4096]{2,1,0:T(8,128)} %bitcast.1, f32[8]{0:T(128)} %skip_ref.1), custom_call_target="tpu_custom_call" | custom-call | tf_op jit(solution)/shard_map/layer/pallas_call | solution.py:551
  115.9 4.5 %copy.9 = bf16[16,131072]{1,0:T(8,128)(2,1)} copy(bf16[16,131072]{1,0:T(8,128)(2,1)} %layer.1) | data formatting | bytes 8388608

commit v4 on v3

--- a/solution.py
+++ b/solution.py
@@ -12,6 +12,7 @@
 Q = 256
 LO = 4
 SPANS = 1 << LO
+STATIC = 3
 SHARD = SPANS * Q
 LOG2E = 1.4426950408889634
 NT = (((1,), (1,)), ((), ()))
@@ -169,7 +170,7 @@
     mix[slot, half:, half:] = jnp.where(tri, low, 0.0).astype(BF16)
 
 
-def span_out(lev, k, r, skip, xb, cb, gb, slow, tiles, shi, ob, mix, slot):
+def span_out(lev, k, low, r, skip, xb, cb, gb, slow, tiles, shi, ob, mix, slot):
     hi = lev - 1 - LO
     at = span_at(k)
     x = xb[r, :, at].astype(F32)
@@ -179,30 +180,38 @@
     xs = (x * tile[1:2, :]).astype(BF16)
     lw = gb[r, :, at].astype(F32)
     acc = dot(xs, mix[slot]) * lw[0:1] + skip * x
-    r_lo = dot_nt(slow[r, k], c)
-    r_hi = dot_nt(shi[r], c)
+    bits = [bit for bit in range(LO) if bit >= STATIC or (low >> bit) & 1]
+    parts = [slow[r, k, bit * P_SIZE : (bit + 1) * P_SIZE, :] for bit in bits] + [shi[r]]
+    terms = dot_nt(jnp.concatenate(parts, axis=0), c)
     e_lo = jnp.exp2(cum)
     e_hi = jnp.exp2(cum + tile[2:3, :])
-    for bit in range(LO):
-        acc = acc + r_lo[bit * P_SIZE : (bit + 1) * P_SIZE] * (lw[1 + bit : 2 + bit] * e_lo)
-    for bit in range(hi):
-        row = 1 + LO + bit
-        acc = acc + r_hi[bit * P_SIZE : (bit + 1) * P_SIZE] * (lw[row : row + 1] * e_hi)
+    rows = [(1 + bit, e_lo) for bit in bits] + [(1 + LO + bit, e_hi) for bit in range(hi)]
+    for n, (row, e) in enumerate(rows):
+        acc = acc + terms[n * P_SIZE : (n + 1) * P_SIZE] * (lw[row : row + 1] * e)
     ob[r, :, at] = acc.astype(BF16)
 
 
 def shard_outputs(lev, r, first, count, skip, xb, bb, cb, gb, slow, tiles, shi, ob, mix):
     span_mix(first, r, bb, cb, tiles, mix, 0)
-
-    def two(m, carry):
-        k = first + 2 * m
-        span_out(lev, k, r, skip, xb, cb, gb, slow, tiles, shi, ob, mix, 0)
-        span_mix(k + 1, r, bb, cb, tiles, mix, 1)
-        span_out(lev, k + 1, r, skip, xb, cb, gb, slow, tiles, shi, ob, mix, 1)
-        span_mix(jnp.minimum(k + 2, first + count - 1), r, bb, cb, tiles, mix, 0)
+    group = 1 << STATIC
+
+    def some(m, carry):
+        base = first + group * m
+        for low in range(group):
+            k = base + low
+            span_out(lev, k, low, r, skip, xb, cb, gb, slow, tiles, shi, ob, mix, low % 2)
+            after = k + 1
+            if low == group - 1:
+                if count == group:
+                    continue
+                after = jnp.minimum(after, first + count - 1)
+            span_mix(after, r, bb, cb, tiles, mix, (low + 1) % 2)
         return carry
 
-    lax.fori_loop(0, count // 2, two, 0)
+    if count == group:
+        some(0, 0)
+    else:
+        lax.fori_loop(0, count // group, some, 0)
 
 
 def kernel(
@@ -550,7 +559,7 @@
     dma = lambda *shape: pltpu.SemaphoreType.DMA(shape)
     return pl.pallas_call(
         functools.partial(kernel, lev, sizes),
-        out_shape=jax.ShapeDtypeStruct((rows, tok), BF16),
+        out_shape=pltpu.VMEM((rows, tok), BF16),
         in_specs=[any_spec, any_spec, any_spec, any_spec, any_spec, any_spec,
                   pl.BlockSpec(memory_space=pltpu.SMEM)],
         out_specs=any_spec,

time: 123 us -> 118 us (0.959); the launches traced: 120 us -> 117 us
  local copies, waits for them, and re-layouts: 4.47 us -> 2.02 us
    unnamed x1, local copies, waits for them, and re-layouts: 4.47 us -> 2.02 us
where the time goes in v4:
time: 118 us; the launch traced here: 117 us
  Pallas kernels  115 us (97%)
  local copies, waits for them, and re-layouts  2.02 us (2%)
    pallas_call x1, Pallas kernels, on_device(): pl.pallas_call(functools.partial(kernel, lev, sizes), out_shape=pltpu.VME...  115 us

profile of v4, /device:TPU:32, one launch (start us, length us, event | category | flops | bytes accessed | tf_op | source)
XLA Modules:
  0.0 117.3 jit_solution(1204618216992390626)
XLA Ops:
  0.0 115.3 %layer.1 = bf16[16,131072]{1,0:T(8,128)(2,1)S(1)} custom-call(bf16[16,131072]{1,0:T(8,128)(2,1)} %x_ref.1, bf16[512,128]{1,0:T(8,128)(2,1)} %b_ref.1, bf16[512,128]{1,0:T(8,128)(2,1)} %c_ref.1, f32[8,4096]{1,0:T(8,128)} %lg_ref.1, f32[8,4096]{1,0:T(8,128)} %st_ref.1, f32[10,8,4096]{2,1,0:T(8,128)} %bitcast.1, f32[8]{0:T(128)} %skip_ref.1), custom_call_target="tpu_custom_call" | custom-call | tf_op jit(solution)/shard_map/layer/pallas_call | solution.py:560
  115.3 2.0 %copy.9 = bf16[16,131072]{1,0:T(8,128)(2,1)} copy(bf16[16,131072]{1,0:T(8,128)(2,1)S(1)} %layer.1) | data formatting | bytes 8388608

commit v5 on v4

--- a/solution.py
+++ b/solution.py
@@ -12,7 +12,8 @@
 Q = 256
 LO = 4
 SPANS = 1 << LO
-STATIC = 3
+STATIC = 2
+GROUP = 1 << STATIC
 SHARD = SPANS * Q
 LOG2E = 1.4426950408889634
 NT = (((1,), (1,)), ((), ()))
@@ -48,7 +49,7 @@
     pk[h] = tmp[...].astype(BF16)
 
 
-def shard_states(lev, r, xb, bb, gb, slow, tiles, g_scr, st_scr):
+def shard_states(lev, r, arrive, xb, bb, gb, slow, tiles, g_scr, st_scr):
     for k in range(SPANS):
         piece = gb[r, :, k * Q : (k + 1) * Q].astype(F32)
         for m in range(3):
@@ -72,6 +73,8 @@
         tiles[r, k, 0:1, :] = cum[k : k + 1]
         tiles[r, k, 1:2, :] = step[k : k + 1]
         tiles[r, k, 2:3, :] = jnp.concatenate([starts[k], starts[k]], axis=1)
+
+    arrive()
 
     def one(k, carry):
         w = xb[r, :, span_at(k)].astype(F32) * g_scr[0, pl.ds(k, 1), :]
@@ -191,27 +194,18 @@
     ob[r, :, at] = acc.astype(BF16)
 
 
-def shard_outputs(lev, r, first, count, skip, xb, bb, cb, gb, slow, tiles, shi, ob, mix):
-    span_mix(first, r, bb, cb, tiles, mix, 0)
-    group = 1 << STATIC
+def shard_outputs(lev, r, skip, flush, xb, bb, cb, gb, slow, tiles, shi, ob, mix):
+    span_mix(0, r, bb, cb, tiles, mix, 0)
 
     def some(m, carry):
-        base = first + group * m
-        for low in range(group):
-            k = base + low
+        for low in range(GROUP):
+            k = GROUP * m + low
             span_out(lev, k, low, r, skip, xb, cb, gb, slow, tiles, shi, ob, mix, low % 2)
-            after = k + 1
-            if low == group - 1:
-                if count == group:
-                    continue
-                after = jnp.minimum(after, first + count - 1)
-            span_mix(after, r, bb, cb, tiles, mix, (low + 1) % 2)
+            span_mix(jnp.minimum(k + 1, SPANS - 1), r, bb, cb, tiles, mix, (low + 1) % 2)
+        flush(m)
         return carry
 
-    if count == group:
-        some(0, 0)
-    else:
-        lax.fori_loop(0, count // group, some, 0)
+    lax.fori_loop(0, SPANS // GROUP, some, 0)
 
 
 def kernel(
@@ -395,7 +389,7 @@
         ref = sums.at[y, r]
         return rc(ref, ref, sent.at[2], r_m.at[0], dev(dy=d))
 
-    part_size = SHARD // 2
+    part_size = GROUP * Q
 
     def out_cols(r, part, yy):
         at = (turn(z + r, nz) * ny + yy) * SHARD + part * part_size
@@ -431,8 +425,9 @@
     def begin(i, carry):
         r = rel(i)
         x_local(r).start()
-        for d in range(1, ny):
-            x_send(r, d).start()
+        for d in (2, 1, 3):
+            if d < ny:
+                x_send(r, d).start()
         return carry
 
     lax.fori_loop(0, nz, begin, 0)
@@ -482,8 +477,8 @@
             def _():
                 g_send(r).wait_recv()
 
-            bulk(xb.at[r], sent.at[0], r_x.at[r]).wait_recv()
-            state, log = shard_states(lev, r, xb, bb, gb, slow, tiles, g_scr, st_scr)
+            arrive = bulk(xb.at[r], sent.at[0], r_x.at[r]).wait_recv
+            state, log = shard_states(lev, r, arrive, xb, bb, gb, slow, tiles, g_scr, st_scr)
             sums[y, r, 0:P_SIZE, :] = state.astype(BF16)
             first = log.astype(BF16).astype(F32)
             rest = log - first
@@ -502,36 +497,33 @@
     skip = skip_ref[z]
     early = min(3, nz)
 
-    def outward(j, carry):
-        i, part = j // 2, lax.rem(j, 2)
+    def outward(i, carry):
         r = rel(i)
 
-        @pl.when(part == 0)
-        def _():
-            @pl.when(i + early < nz)
-            def _():
-                step_a(1, i + early)
-
-            @pl.when(i + 2 < nz)
-            def _():
-                step_b(1, i + 2)
-
-            @pl.when(i + 1 < nz)
-            def _():
-                step_c(1, i + 1)
-
-            step_s(1, i)
-
-        half = SPANS // 2
-        shard_outputs(
-            lev, r, part * half, half, skip, xb, bb, cb, gb, slow, tiles, shi, ob, mix
-        )
-        o_local(r, part).start()
-        for d in range(1, ny):
-            o_send(r, part, d).start()
+        @pl.when(i + early < nz)
+        def _():
+            step_a(1, i + early)
+
+        @pl.when(i + 2 < nz)
+        def _():
+            step_b(1, i + 2)
+
+        @pl.when(i + 1 < nz)
+        def _():
+            step_c(1, i + 1)
+
+        step_s(1, i)
+
+        def flush(part):
+            for d in (2, 1, 3):
+                if d < ny:
+                    o_send(r, part, d).start()
+            o_local(r, part).start()
+
+        shard_outputs(lev, r, skip, flush, xb, bb, cb, gb, slow, tiles, shi, ob, mix)
         return carry
 
-    lax.fori_loop(0, 2 * nz, outward, 0)
+    lax.fori_loop(0, nz, outward, 0)
 
     away = nz * (ny - 1) * rows * SHARD // (P_SIZE * SHARD)
     bulk(xb.at[pl.ds(0, away)], sent.at[0], r_x.at[0]).wait_send()

time: 118 us -> 117 us (level)
  no operation moved by 1% of the time
where the time goes in v5:
time: 117 us
  Pallas kernels  114 us (97%)
  local copies, waits for them, and re-layouts  2.02 us (2%)
    pallas_call x1, Pallas kernels, on_device(): pl.pallas_call(functools.partial(kernel, lev, sizes), out_shape=pltpu.VME...  114 us

profile of v5, /device:TPU:32, one launch (start us, length us, event | category | flops | bytes accessed | tf_op | source)
XLA Modules:
  0.0 116.5 jit_solution(10613214870208449191)
XLA Ops:
  0.0 114.5 %layer.1 = bf16[16,131072]{1,0:T(8,128)(2,1)S(1)} custom-call(bf16[16,131072]{1,0:T(8,128)(2,1)} %x_ref.1, bf16[512,128]{1,0:T(8,128)(2,1)} %b_ref.1, bf16[512,128]{1,0:T(8,128)(2,1)} %c_ref.1, f32[8,4096]{1,0:T(8,128)} %lg_ref.1, f32[8,4096]{1,0:T(8,128)} %st_ref.1, f32[10,8,4096]{2,1,0:T(8,128)} %bitcast.1, f32[8]{0:T(128)} %skip_ref.1), custom_call_target="tpu_custom_call" | custom-call | tf_op jit(solution)/shard_map/layer/pallas_call | solution.py:552
  114.5 2.0 %copy.9 = bf16[16,131072]{1,0:T(8,128)(2,1)} copy(bf16[16,131072]{1,0:T(8,128)(2,1)S(1)} %layer.1) | data formatting | bytes 8388608
